TPU v7x, 32 devices: a whole 2x2x4 slice. The times are simulated.
32 devices in a mesh: block: 4 (over y, x), tok: 8 (over z, core).
Axes of the slice: x: 2, y: 2, z: 4, core: 2. Of those that a mesh axis runs over, the one named last changes fastest.
Arguments:
- queries: float32 [4096, 256], P(('block', 'tok')), may hold values from -6 to 6
- keys: float32 [4096, 256], P(('block', 'tok')), may hold values from -6 to 6
- values: float32 [4096, 256], P(('block', 'tok')), may hold values from -6 to 6
- rates: float32 [4096], P(('block', 'tok')), may hold values from 0.0001 to 0.001
- states: float32 [4, 3, 256, 256], P('block', None, 'tok'), may hold values from -0.375 to 0.375
- out_cot: float32 [4096, 256], P(('block', 'tok')), may hold values from -6 to 6
- final_cot: float32 [3, 256, 256], P(None, 'tok'), may hold values from -6 to 6
Outputs:
- d_queries: float32 [4096, 256], P(('block', 'tok'))
- d_keys: float32 [4096, 256], P(('block', 'tok'))
- d_values: float32 [4096, 256], P(('block', 'tok'))
- d_rates: float32 [4096], P(('block', 'tok'))
- d_states: float32 [4, 3, 256, 256], P('block', None, 'tok')
All inputs are finite; a program needn't handle non-finite values.
Results may differ from a plain program's by a relative error of at most 0.00029.
Values sent between devices are 32-bit elements; how exact they have to be, the bound alone decides.
No kernel may reach another device: no remote copies, remote signals or barrier semaphores. Data moves between devices by JAX's collectives and lax.ppermute only.
A program may use at most 64 MiB of HBM per device.

v0:
```python
import jax
import jax.numpy as jnp
from jax import lax
from jax.sharding import PartitionSpec as P

EPS = 1e-06
HIGH = lax.Precision.HIGHEST


def from_behind(array, axis, by):
    devices = lax.axis_size(axis)
    pairs = [(i, i + by) for i in range(devices) if 0 <= i + by < devices]
    return lax.ppermute(array, axis, pairs)


def apply_fast(weights, inputs):
    first = jnp.dot(inputs, weights[0], precision=HIGH, preferred_element_type=jnp.float32)
    gate = jnp.dot(inputs, weights[1], precision=HIGH, preferred_element_type=jnp.float32)
    mixed = jax.nn.silu(first) * gate
    return jnp.dot(mixed, weights[2], precision=HIGH, preferred_element_type=jnp.float32)


def update_grad(weights, keys, values, rates):

    def loss(current):
        return -jnp.sum(rates[:, None] * apply_fast(current, keys) * values)

    return jax.grad(loss)(weights)


def norm_adjoint(incoming, shifted, own, row_norm, new_norm):
    inner = jnp.sum(incoming * shifted, axis=-1, keepdims=True)
    d_shifted = (
        row_norm / new_norm * incoming
        - row_norm * inner / (new_norm * new_norm * new_norm) * shifted
    )
    direct = d_shifted + inner / new_norm * own / row_norm
    return (d_shifted, direct)


def per_device(queries, keys, values, rates, states, out_cot, final_cot):
    groups = lax.axis_size("block")
    position = lax.axis_index("block")
    own_rows = states[0]
    gathered = lax.all_gather(own_rows, "tok", axis=1, tiled=True)
    _, apply_back = jax.vjp(apply_fast, gathered, queries)
    apply_state, d_queries = apply_back(out_cot)
    grad_part, second_back = jax.vjp(update_grad, gathered, keys, values, rates)
    grad_rows = lax.psum_scatter(grad_part, "tok", scatter_dimension=1, tiled=True)
    shifted = own_rows - grad_rows
    row_norm = jnp.sqrt(jnp.sum(own_rows * own_rows, axis=-1, keepdims=True) + EPS)
    new_norm = jnp.sqrt(jnp.sum(shifted * shifted, axis=-1, keepdims=True) + EPS)
    zero_back = (
        jnp.zeros_like(gathered),
        jnp.zeros_like(keys),
        jnp.zeros_like(values),
        jnp.zeros_like(rates),
    )
    incoming = final_cot
    d_keys = jnp.zeros_like(keys)
    d_values = jnp.zeros_like(values)
    d_rates = jnp.zeros_like(rates)
    d_rows = jnp.zeros_like(own_rows)
    for section in range(groups):
        active = position == groups - 1 - section
        d_shifted, direct = norm_adjoint(incoming, shifted, own_rows, row_norm, new_norm)
        d_grad = lax.all_gather(-d_shifted, "tok", axis=1, tiled=True)
        second_state, second_keys, second_values, second_rates = lax.cond(
            active, lambda cot: second_back(cot), lambda cot: zero_back, d_grad
        )
        summed = lax.psum_scatter(
            second_state + apply_state, "tok", scatter_dimension=1, tiled=True
        )
        rows_now = summed + direct
        d_keys = jnp.where(active, second_keys, d_keys)
        d_values = jnp.where(active, second_values, d_values)
        d_rates = jnp.where(active, second_rates, d_rates)
        d_rows = jnp.where(active, rows_now, d_rows)
        if section + 1 < groups:
            incoming = from_behind(rows_now, "block", -1)
    return (d_queries, d_keys, d_values, d_rates, d_rows[None])


def solution(mesh):
    return jax.shard_map(
        per_device,
        mesh=mesh,
        in_specs=(
            P(("block", "tok"), None),
            P(("block", "tok"), None),
            P(("block", "tok"), None),
            P(("block", "tok")),
            P("block", None, "tok", None),
            P(("block", "tok"), None),
            P(None, "tok", None),
        ),
        out_specs=(
            P(("block", "tok"), None),
            P(("block", "tok"), None),
            P(("block", "tok"), None),
            P(("block", "tok")),
            P("block", None, "tok", None),
        ),
        check_vma=False,
    )
```

profile of v0, /device:TPU:0, one launch (start us, length us, event | category | flops | bytes accessed | tf_op | source)
XLA Modules:
  0.0 317.6 jit_solution(9422228278440571591)
XLA Ops:
  7.9 17.5 %all-gather = f32[1,3,256,256]{3,2,1,0:T(8,128)S(1)} all-gather(f32[1,3,32,256]{3,2,1,0:T(8,128)} %param.19), channel_id=2, replica_groups=mesh['block'=4,'tok'=8] {'tok'}, dimensions={2}, use_global_device_ids=true | all-gather | bytes 884736 | tf_op jit(solution)/shard_map/all_gather | solution.py:45
  27.1 1.1 multiply_add_fusion.12
  34.6 29.1 %reduce-scatter.6.cloned.1.call-done = f32[3,32,256]{2,1,0:T(8,128)} async-done(((f32[3,256,256]{2,1,0:T(8,128)}), f32[3,32,256]{2,1,0:T(8,128)}) %reduce-scatter.6.cloned.1.call-update) | async-done | bytes 98320 | tf_op jit(solution)/shard_map/reduce_scatter | solution.py:49
  63.7 1.1 multiply_reduce_fusion.8
  65.0 15.9 %all_gather.16 = f32[3,256,256]{2,1,0:T(8,128)S(1)} all-gather(f32[3,32,256]{2,1,0:T(8,128)S(1)} %fusion.92), channel_id=1, replica_groups=mesh['block'=4,'tok'=8] {'tok'}, dimensions={1}, use_global_device_ids=true | all-gather | bytes 884736 | tf_op jit(solution)/shard_map/all_gather | solution.py:67
  81.5 1.4 conditional.4
  83.9 35.0 %reduce-scatter.8.cloned.1.call-done = f32[3,32,256]{2,1,0:T(8,128)} async-done(((f32[3,256,256]{2,1,0:T(8,128)}), f32[3,32,256]{2,1,0:T(8,128)}) %reduce-scatter.8.cloned.1.call-update) | async-done | bytes 98320 | tf_op jit(solution)/shard_map/reduce_scatter | solution.py:71
  118.9 1.7 fusion.76
  120.6 1.3 collective-permute-start
  121.9 5.5 %collective-permute-done = f32[3,32,256]{2,1,0:T(8,128)} collective-permute-done((f32[3,32,256]{2,1,0:T(8,128)}, f32[3,32,256]{2,1,0:T(8,128)}, u32[]{:S(2)}, u32[]{:S(2)}) %collective-permute-start) | collective-permute-done | bytes 98336 | tf_op jit(solution)/shard_map/ppermute | solution.py:13
  128.5 1.0 fusion.93
  129.6 15.8 %all_gather.17 = f32[3,256,256]{2,1,0:T(8,128)S(1)} all-gather(f32[3,32,256]{2,1,0:T(8,128)S(1)} %fusion.93), channel_id=1, replica_groups=mesh['block'=4,'tok'=8] {'tok'}, dimensions={1}, use_global_device_ids=true | all-gather | bytes 884736 | tf_op jit(solution)/shard_map/all_gather | solution.py:67
  145.4 1.6 conditional.5
  148.1 34.5 %reduce-scatter.10.cloned.1.call-done = f32[3,32,256]{2,1,0:T(8,128)} async-done(((f32[3,256,256]{2,1,0:T(8,128)}), f32[3,32,256]{2,1,0:T(8,128)}) %reduce-scatter.10.cloned.1.call-update) | async-done | bytes 98320 | tf_op jit(solution)/shard_map/reduce_scatter | solution.py:71
  182.6 1.7 fusion.79
  184.3 1.3 collective-permute-start.1
  185.6 5.5 %collective-permute-done.1 = f32[3,32,256]{2,1,0:T(8,128)} collective-permute-done((f32[3,32,256]{2,1,0:T(8,128)}, f32[3,32,256]{2,1,0:T(8,128)}, u32[]{:S(2)}, u32[]{:S(2)}) %collective-permute-start.1) | collective-permute-done | bytes 98336 | tf_op jit(solution)/shard_map/ppermute | solution.py:13
  192.2 1.0 fusion.94
  193.2 15.8 %all_gather.18 = f32[3,256,256]{2,1,0:T(8,128)S(1)} all-gather(f32[3,32,256]{2,1,0:T(8,128)S(1)} %fusion.94), channel_id=1, replica_groups=mesh['block'=4,'tok'=8] {'tok'}, dimensions={1}, use_global_device_ids=true | all-gather | bytes 884736 | tf_op jit(solution)/shard_map/all_gather | solution.py:67
  209.1 1.4 conditional.6
  211.5 35.1 %reduce-scatter.12.cloned.1.call-done = f32[3,32,256]{2,1,0:T(8,128)} async-done(((f32[3,256,256]{2,1,0:T(8,128)}), f32[3,32,256]{2,1,0:T(8,128)}) %reduce-scatter.12.cloned.1.call-update) | async-done | bytes 98320 | tf_op jit(solution)/shard_map/reduce_scatter | solution.py:71
  246.6 1.7 fusion.82
  248.3 1.3 collective-permute-start.2
  249.6 5.5 %collective-permute-done.2 = f32[3,32,256]{2,1,0:T(8,128)} collective-permute-done((f32[3,32,256]{2,1,0:T(8,128)}, f32[3,32,256]{2,1,0:T(8,128)}, u32[]{:S(2)}, u32[]{:S(2)}) %collective-permute-start.2) | collective-permute-done | bytes 98336 | tf_op jit(solution)/shard_map/ppermute | solution.py:13
  256.2 1.0 fusion.95
  257.3 15.8 %all_gather.19 = f32[3,256,256]{2,1,0:T(8,128)S(1)} all-gather(f32[3,32,256]{2,1,0:T(8,128)S(1)} %fusion.95), channel_id=1, replica_groups=mesh['block'=4,'tok'=8] {'tok'}, dimensions={1}, use_global_device_ids=true | all-gather | bytes 884736 | tf_op jit(solution)/shard_map/all_gather | solution.py:67
  273.1 6.2 %conditional.7 = (f32[3,256,256]{2,1,0:T(8,128)S(1)}, f32[128,256]{1,0:T(8,128)}, f32[128,256]{1,0:T(8,128)}, f32[128]{0:T(128)S(1)}) conditional(s32[]{:T(128)} %convert_element_type.12, () %tuple.51, (f32[3,256,256]{2,1,0:T(8,128)S(1)}, f32[128,256]{1,0:T(8,128)S(1)}, f32[128,256]{1,0:T(8,128)S(1)}, f32[128,256]{1,0:T(8,128)S(1)}, ...), branch_computations={%region_19.20_spmd, %region_20.22_spmd} | conditional | flops 1209499520 | bytes 10880032 | solution.py:68
  276.9 1.1 convolution_add_fusion.13
  282.1 1.0 convolution_add_fusion.16
  283.7 1.7 select_select_fusion
  285.4 23.9 %reduce-scatter.14.cloned.1.call-done = f32[3,32,256]{2,1,0:T(8,128)} async-done(((f32[3,256,256]{2,1,0:T(8,128)}), f32[3,32,256]{2,1,0:T(8,128)}) %reduce-scatter.14.cloned.1.call-update) | async-done | bytes 98320 | tf_op jit(solution)/shard_map/reduce_scatter | solution.py:71
  309.3 1.7 fusion.72
  (154 shorter events, 27.9 us)
Async XLA Ops:
  7.2 23.4 %copy-start = (f32[128,256]{1,0:T(8,128)S(1)}, f32[128,256]{1,0:T(8,128)}, u32[]{:S(2)}) copy-start(f32[128,256]{1,0:T(8,128)} %param.15) | copy-start | bytes 393220
  7.2 56.5 %reduce-scatter.6.cloned.1.call-start = ((), (), s32[]{:S(2)}) async-start(), calls=%async_computation.5 | async-start | bytes 884736 | tf_op jit(solution)/shard_map/reduce_scatter | solution.py:49
  7.9 17.6 %copy-start.43 = (f32[128,256]{1,0:T(8,128)S(1)}, f32[128,256]{1,0:T(8,128)}, u32[]{:S(2)}) copy-start(f32[128,256]{1,0:T(8,128)} %param.17) | copy-start | bytes 393220
  30.5 88.4 %reduce-scatter.8.cloned.1.call-start = ((), (), s32[]{:S(2)}) async-start(), calls=%async_computation.6 | async-start | bytes 884736 | tf_op jit(solution)/shard_map/reduce_scatter | solution.py:71
  33.7 30.0 %copy-start.20 = (f32[1,3,32,256]{3,2,1,0:T(8,128)S(1)}, f32[1,3,32,256]{3,2,1,0:T(8,128)}, u32[]{:S(2)}) copy-start(f32[1,3,32,256]{3,2,1,0:T(8,128)} %param.19) | copy-start | bytes 294916
  63.7 17.2 %copy-start.33 = (f32[128,256]{1,0:T(8,128)S(1)}, f32[128,256]{1,0:T(8,128)}, u32[]{:S(2)}) copy-start(f32[128,256]{1,0:T(8,128)} %get-tuple-element.291) | copy-start | bytes 393220
  64.8 16.0 %copy-start.21 = (f32[128,256]{1,0:T(8,128)S(1)}, f32[128,256]{1,0:T(8,128)}, u32[]{:S(2)}) copy-start(f32[128,256]{1,0:T(8,128)} %get-tuple-element.312) | copy-start | bytes 393220
  64.8 16.0 %copy-start.25 = (f32[128,256]{1,0:T(8,128)S(1)}, f32[128,256]{1,0:T(8,128)}, u32[]{:S(2)}) copy-start(f32[128,256]{1,0:T(8,128)} %get-tuple-element.314) | copy-start | bytes 393220
  64.8 16.0 %copy-start.29 = (f32[128,256]{1,0:T(8,128)S(1)}, f32[128,256]{1,0:T(8,128)}, u32[]{:S(2)}) copy-start(f32[128,256]{1,0:T(8,128)} %get-tuple-element.315) | copy-start | bytes 393220
  64.9 15.9 %copy-start.2 = (f32[256,256]{1,0:T(8,128)S(1)}, f32[256,256]{1,0:T(8,128)}, u32[]{:S(2)}) copy-start(f32[256,256]{1,0:T(8,128)} %get-tuple-element.308) | copy-start | bytes 786436
  64.9 15.9 %copy-start.6 = (f32[256,256]{1,0:T(8,128)S(1)}, f32[256,256]{1,0:T(8,128)}, u32[]{:S(2)}) copy-start(f32[256,256]{1,0:T(8,128)} %get-tuple-element.309) | copy-start | bytes 786436
  64.9 15.9 %copy-start.11 = (f32[128,256]{1,0:T(8,128)S(1)}, f32[128,256]{1,0:T(8,128)}, u32[]{:S(2)}) copy-start(f32[128,256]{1,0:T(8,128)} %copy-done.10) | copy-start | bytes 393220
  65.0 15.9 %copy-start.16 = (f32[128,256]{1,0:T(8,128)S(1)}, f32[128,256]{1,0:T(8,128)}, u32[]{:S(2)}) copy-start(f32[128,256]{1,0:T(8,128)} %copy-done.15) | copy-start | bytes 393220
  83.9 98.7 %reduce-scatter.10.cloned.1.call-start = ((), (), s32[]{:S(2)}) async-start(), calls=%async_computation.7 | async-start | bytes 884736 | tf_op jit(solution)/shard_map/reduce_scatter | solution.py:71
  120.6 6.8 %collective-permute-start = (f32[3,32,256]{2,1,0:T(8,128)}, f32[3,32,256]{2,1,0:T(8,128)}, u32[]{:S(2)}, u32[]{:S(2)}) collective-permute-start(f32[3,32,256]{2,1,0:T(8,128)} %fusion.76), channel_id=1, source_target_pairs={{8,0},{16,8},{24,16},{9,1},{17,9},{25,17},{10,2},{18,10},{26,18},{... | collective-permute-start | bytes 294920 | tf_op jit(solution)/shard_map/ppermute | solution.py:13
  127.4 17.9 %copy-start.34 = (f32[128,256]{1,0:T(8,128)S(1)}, f32[128,256]{1,0:T(8,128)}, u32[]{:S(2)}) copy-start(f32[128,256]{1,0:T(8,128)} %get-tuple-element.291) | copy-start | bytes 393220
  128.5 16.9 %copy-start.22 = (f32[128,256]{1,0:T(8,128)S(1)}, f32[128,256]{1,0:T(8,128)}, u32[]{:S(2)}) copy-start(f32[128,256]{1,0:T(8,128)} %get-tuple-element.312) | copy-start | bytes 393220
  128.5 16.9 %copy-start.26 = (f32[128,256]{1,0:T(8,128)S(1)}, f32[128,256]{1,0:T(8,128)}, u32[]{:S(2)}) copy-start(f32[128,256]{1,0:T(8,128)} %get-tuple-element.314) | copy-start | bytes 393220
  128.5 16.9 %copy-start.30 = (f32[128,256]{1,0:T(8,128)S(1)}, f32[128,256]{1,0:T(8,128)}, u32[]{:S(2)}) copy-start(f32[128,256]{1,0:T(8,128)} %get-tuple-element.315) | copy-start | bytes 393220
  129.6 15.8 %copy-start.3 = (f32[256,256]{1,0:T(8,128)S(1)}, f32[256,256]{1,0:T(8,128)}, u32[]{:S(2)}) copy-start(f32[256,256]{1,0:T(8,128)} %get-tuple-element.308) | copy-start | bytes 786436
  148.1 98.6 %reduce-scatter.12.cloned.1.call-start = ((), (), s32[]{:S(2)}) async-start(), calls=%async_computation.8 | async-start | bytes 884736 | tf_op jit(solution)/shard_map/reduce_scatter | solution.py:71
  184.3 6.8 %collective-permute-start.1 = (f32[3,32,256]{2,1,0:T(8,128)}, f32[3,32,256]{2,1,0:T(8,128)}, u32[]{:S(2)}, u32[]{:S(2)}) collective-permute-start(f32[3,32,256]{2,1,0:T(8,128)} %fusion.79), channel_id=1, source_target_pairs={{8,0},{16,8},{24,16},{9,1},{17,9},{25,17},{10,2},{18,10},{26,18},{... | collective-permute-start | bytes 294920 | tf_op jit(solution)/shard_map/ppermute | solution.py:13
  191.1 17.9 %copy-start.35 = (f32[128,256]{1,0:T(8,128)S(1)}, f32[128,256]{1,0:T(8,128)}, u32[]{:S(2)}) copy-start(f32[128,256]{1,0:T(8,128)} %get-tuple-element.291) | copy-start | bytes 393220
  192.1 16.9 %copy-start.23 = (f32[128,256]{1,0:T(8,128)S(1)}, f32[128,256]{1,0:T(8,128)}, u32[]{:S(2)}) copy-start(f32[128,256]{1,0:T(8,128)} %get-tuple-element.312) | copy-start | bytes 393220
  192.1 16.9 %copy-start.27 = (f32[128,256]{1,0:T(8,128)S(1)}, f32[128,256]{1,0:T(8,128)}, u32[]{:S(2)}) copy-start(f32[128,256]{1,0:T(8,128)} %get-tuple-element.314) | copy-start | bytes 393220
  192.2 16.9 %copy-start.31 = (f32[128,256]{1,0:T(8,128)S(1)}, f32[128,256]{1,0:T(8,128)}, u32[]{:S(2)}) copy-start(f32[128,256]{1,0:T(8,128)} %get-tuple-element.315) | copy-start | bytes 393220
  211.5 97.8 %reduce-scatter.14.cloned.1.call-start = ((), (), s32[]{:S(2)}) async-start(), calls=%async_computation.9 | async-start | bytes 884736 | tf_op jit(solution)/shard_map/reduce_scatter | solution.py:71
  248.3 6.8 %collective-permute-start.2 = (f32[3,32,256]{2,1,0:T(8,128)}, f32[3,32,256]{2,1,0:T(8,128)}, u32[]{:S(2)}, u32[]{:S(2)}) collective-permute-start(f32[3,32,256]{2,1,0:T(8,128)} %fusion.82), channel_id=1, source_target_pairs={{8,0},{16,8},{24,16},{9,1},{17,9},{25,17},{10,2},{18,10},{26,18},{... | collective-permute-start | bytes 294920 | tf_op jit(solution)/shard_map/ppermute | solution.py:13
  255.1 17.9 %copy-start.36 = (f32[128,256]{1,0:T(8,128)S(1)}, f32[128,256]{1,0:T(8,128)}, u32[]{:S(2)}) copy-start(f32[128,256]{1,0:T(8,128)} %get-tuple-element.291) | copy-start | bytes 393220
  256.2 16.9 %copy-start.24 = (f32[128,256]{1,0:T(8,128)S(1)}, f32[128,256]{1,0:T(8,128)}, u32[]{:S(2)}) copy-start(f32[128,256]{1,0:T(8,128)} %get-tuple-element.312) | copy-start | bytes 393220
  256.2 16.9 %copy-start.28 = (f32[128,256]{1,0:T(8,128)S(1)}, f32[128,256]{1,0:T(8,128)}, u32[]{:S(2)}) copy-start(f32[128,256]{1,0:T(8,128)} %get-tuple-element.314) | copy-start | bytes 393220
  256.2 16.9 %copy-start.32 = (f32[128,256]{1,0:T(8,128)S(1)}, f32[128,256]{1,0:T(8,128)}, u32[]{:S(2)}) copy-start(f32[128,256]{1,0:T(8,128)} %get-tuple-element.315) | copy-start | bytes 393220
  (21 other events, 183.2 us)
Sparse Core Ops, SparseCore 0:
  30.6 33.0 reduce-scatter.5
  84.0 34.8 reduce-scatter.7
  148.2 34.3 reduce-scatter.9
  211.6 34.9 reduce-scatter.11
  280.4 28.8 reduce-scatter.13
where the time goes:
time: 318 us
  waiting for transfers between devices  174 us (55%)
  blocking collectives  80.7 us (25%)
  other arithmetic  22.3 us (7%)
  between operations  14.5 us (5%)
  matrix products  12.5 us (4%)
  local copies, waits for them, and re-layouts  8.76 us (3%)
  starting transfers between devices  4.04 us (1%)
    reduce_scatter x4, waiting for transfers between devices, per_device(): lax.psum_scatter(second_state + apply_state, 'tok', scatter_dimension=1,...  128 us
    all_gather x4, blocking collectives, per_device(): d_grad = lax.all_gather(-d_shifted, 'tok', axis=1, tiled=True)  63.2 us
    reduce_scatter x1, waiting for transfers between devices, per_device(): lax.psum_scatter(grad_part, 'tok', scatter_dimension=1, tiled=True)  29.1 us
    all_gather x1, blocking collectives, per_device(): gathered = lax.all_gather(own_rows, 'tok', axis=1, tiled=True)  17.5 us
    ppermute x3, waiting for transfers between devices, from_behind(): return lax.ppermute(array, axis, pairs)  16.6 us
  transfers between devices with their start and end apart: 8, of which 8 were waited for; matrix products, arithmetic and copies ran while one was open for 2% of the time, Pallas kernels for 0%

commit v1 on v0

v1 whole, which is shorter than its diff:
```python
import jax
import jax.numpy as jnp
from jax import lax
from jax.sharding import PartitionSpec as P

EPS = 1e-06
HIGH = lax.Precision.HIGHEST


def mm(left, right):
    return lax.dot_general(left, right, (((1,), (0,)), ((), ())), precision=HIGH, preferred_element_type=jnp.float32)


def mm_nt(left, right):
    return lax.dot_general(left, right, (((1,), (1,)), ((), ())), precision=HIGH, preferred_element_type=jnp.float32)


def mm_tn(left, right):
    return lax.dot_general(left, right, (((0,), (0,)), ((), ())), precision=HIGH, preferred_element_type=jnp.float32)


def silu_parts(first):
    sig = 1.0 / (1.0 + jnp.exp(-first))
    slope = sig * (1.0 - sig)
    value = first * sig
    d_one = sig + first * slope
    d_two = slope * (2.0 + first * (1.0 - 2.0 * sig))
    return value, d_one, d_two


def direct(size):
    return size % 2 == 0 and size <= 16


def chip_shift(array, by):
    size = lax.axis_size("tok")
    return lax.ppermute(array, "tok", [(j, (j + 2 * by) % size) for j in range(size)])


def core_swap(array):
    size = lax.axis_size("tok")
    return lax.ppermute(array, "tok", [(j, j ^ 1) for j in range(size)])


def gather_pieces(array):
    size = lax.axis_size("tok")
    if not direct(size):
        return lax.all_gather(array, "tok")
    mine = jnp.stack([array] + [chip_shift(array, by) for by in range(1, size // 2)])
    return jnp.concatenate([mine, core_swap(mine)])


def spread_sum(pieces):
    size = lax.axis_size("tok")
    if not direct(size):
        return lax.psum_scatter(pieces, "tok")
    half = size // 2
    mine = pieces[:half] + core_swap(pieces[half:])
    total = mine[0]
    for by in range(1, half):
        total = total + chip_shift(mine[by], -by)
    return total


def sum_all(array):
    size = lax.axis_size("tok")
    if not direct(size):
        return jnp.sum(lax.all_gather(array, "tok"), axis=0)
    array = array + core_swap(array)
    total = array
    for by in range(1, size // 2):
        total = total + chip_shift(array, by)
    return total


def rows_to_hidden(rows):
    size = lax.axis_size("tok")
    count, depth, width = rows.shape
    parts = rows.reshape(count, depth, size, width // size).transpose(2, 0, 3, 1)
    parts = lax.all_to_all(parts, "tok", 0, 0)
    return parts.transpose(1, 2, 0, 3).reshape(count, width // size, depth * size)


def hidden_to_rows(slices):
    size = lax.axis_size("tok")
    count, depth, width = slices.shape
    parts = slices.reshape(count, depth, size, width // size).transpose(2, 0, 1, 3)
    parts = lax.all_to_all(parts, "tok", 0, 0)
    return parts.transpose(1, 3, 0, 2).reshape(count, width // size, depth * size)


def to_block(array, source, target, by=0):
    size = lax.axis_size("tok")
    pairs = [(source * size + j, target * size + (j + by) % size) for j in range(size)]
    return lax.ppermute(array, ("block", "tok"), pairs)


def up_one(array):
    groups = lax.axis_size("block")
    return lax.ppermute(array, "block", [(i, i + 1) for i in range(groups - 1)])


def slice_forward(weights, keys, scaled):
    first, gate = mm_nt(weights[0], keys), mm_nt(weights[1], keys)
    value, d_one, d_two = silu_parts(first)
    d_mixed = mm_nt(weights[2], scaled)
    mixed = value * gate
    d_gate = d_mixed * value
    d_first = d_mixed * gate * d_one
    grads = jnp.stack([mm(d_first, keys), mm(d_gate, keys), mm(mixed, scaled)])
    return grads, (gate, value, d_one, d_two, d_mixed)


def slice_adjoint(cot, kept, keys, scaled):
    gate, value, d_one, d_two, d_mixed = kept
    t_first, t_gate, p_mixed = mm_nt(cot[0], keys), mm_nt(cot[1], keys), mm_nt(cot[2], scaled)
    t_mixed = d_one * t_first * gate + value * t_gate
    c_gate = p_mixed * value + d_mixed * d_one * t_first
    c_first = p_mixed * gate * d_one + d_mixed * (d_two * t_first * gate + d_one * t_gate)
    return jnp.stack([mm(c_first, keys), mm(c_gate, keys), mm(t_mixed, scaled)])


def query_adjoint(weights, queries, out_cot):
    first, gate = mm_nt(queries, weights[0]), mm_nt(queries, weights[1])
    value, d_one, _ = silu_parts(first)
    d_mixed = mm_nt(out_cot, weights[2])
    d_gate = d_mixed * value
    d_first = d_mixed * gate * d_one
    d_queries = mm(d_first, weights[0]) + mm(d_gate, weights[1])
    d_weights = jnp.stack([mm_tn(d_first, queries), mm_tn(d_gate, queries), mm_tn(value * gate, out_cot)])
    return d_queries, d_weights


def token_adjoint(weights, cot, keys, scaled):
    first, gate = mm_nt(keys, weights[0]), mm_nt(keys, weights[1])
    value, d_one, d_two = silu_parts(first)
    d_mixed = mm_nt(scaled, weights[2])
    mixed = value * gate
    d_gate = d_mixed * value
    d_first = d_mixed * gate * d_one
    t_first, t_gate, p_mixed = mm_nt(keys, cot[0]), mm_nt(keys, cot[1]), mm_nt(scaled, cot[2])
    t_mixed = d_one * t_first * gate + value * t_gate
    c_gate = p_mixed * value + d_mixed * d_one * t_first
    c_first = p_mixed * gate * d_one + d_mixed * (d_two * t_first * gate + d_one * t_gate)
    d_keys = mm(c_first, weights[0]) + mm(c_gate, weights[1]) + mm(d_first, cot[0]) + mm(d_gate, cot[1])
    t_out = mm(t_mixed, weights[2]) + mm(mixed, cot[2])
    return d_keys, t_out


def over_hidden(array):
    return jnp.sum(array[:2], axis=1)


def per_device(queries, keys, values, rates, states, out_cot, final_cot):
    groups, size = lax.axis_size("block"), lax.axis_size("tok")
    position = lax.axis_index("block")
    own_rows = states[0]
    scaled = -rates[:, None] * values
    both = gather_pieces(jnp.stack([keys, scaled]))
    width = keys.shape[1]
    all_keys = both[:, 0].reshape(-1, width)
    all_scaled = both[:, 1].reshape(-1, width)
    split = rows_to_hidden(jnp.concatenate([own_rows[:2], final_cot[:2]]))
    own = jnp.concatenate([split[:2], own_rows[2:]])
    last = jnp.concatenate([split[2:], final_cot[2:]])
    grads, kept = slice_forward(own, all_keys, all_scaled)
    shifted = own - grads
    earlier = up_one(shifted[:2])
    sums = sum_all(jnp.concatenate([over_hidden(own * own), over_hidden(shifted * shifted), over_hidden(last * shifted)]))
    row_norm = [jnp.sqrt(sums[0:2, None, :] + EPS), jnp.sqrt(jnp.sum(own[2:] ** 2, axis=-1, keepdims=True) + EPS)]
    new_norm = [jnp.sqrt(sums[2:4, None, :] + EPS), jnp.sqrt(jnp.sum(shifted[2:] ** 2, axis=-1, keepdims=True) + EPS)]

    pieces = gather_pieces(own)
    whole = pieces.transpose(1, 0, 2, 3).reshape(3, -1, width)
    d_queries, d_weights = query_adjoint(whole, queries, out_cot)
    apply_state = spread_sum(d_weights.reshape(3, size, -1, width).transpose(1, 0, 2, 3))

    is_last = position == groups - 1
    incoming = jnp.where(is_last, last, 0.0)
    inner = jnp.where(is_last, sums[4:6], 0.0)
    for section in range(groups):
        inners = [inner[:, None, :], jnp.sum(incoming[2:] * shifted[2:], axis=-1, keepdims=True)]
        cots, straights = [], []
        for part, dot, old, new in zip((slice(0, 2), slice(2, 3)), inners, row_norm, new_norm):
            d_shifted = old / new * incoming[part] - old * dot / (new * new * new) * shifted[part]
            cots.append(-d_shifted)
            straights.append(d_shifted + dot / new * own[part] / old)
        cot = jnp.concatenate(cots)
        straight = jnp.concatenate(straights)
        rows_now = slice_adjoint(cot, kept, all_keys, all_scaled) + apply_state + straight
        if section + 1 < groups:
            source = groups - 1 - section
            partial = over_hidden(rows_now[:2] * earlier)
            incoming = incoming + to_block(rows_now, source, source - 1)
            if direct(size):
                for by in range(size):
                    inner = inner + to_block(partial, source, source - 1, by)
            else:
                inner = inner + to_block(sum_all(partial), source, source - 1)
    cot_pieces = gather_pieces(cot)
    whole_cot = cot_pieces.transpose(1, 0, 2, 3).reshape(3, -1, width)
    d_keys, t_out = token_adjoint(whole, whole_cot, keys, scaled)
    d_values = -rates[:, None] * t_out
    d_rates = -jnp.sum(values * t_out, axis=-1)
    d_rows = jnp.concatenate([hidden_to_rows(rows_now[:2]), rows_now[2:]])
    return (d_queries, d_keys, d_values, d_rates, d_rows[None])


def solution(mesh):
    return jax.shard_map(
        per_device,
        mesh=mesh,
        in_specs=(
            P(("block", "tok"), None),
            P(("block", "tok"), None),
            P(("block", "tok"), None),
            P(("block", "tok")),
            P("block", None, "tok", None),
            P(("block", "tok"), None),
            P(None, "tok", None),
        ),
        out_specs=(
            P(("block", "tok"), None),
            P(("block", "tok"), None),
            P(("block", "tok"), None),
            P(("block", "tok")),
            P("block", None, "tok", None),
        ),
        check_vma=False,
    )
```

time: 318 us -> 186 us (0.58)
  waiting for transfers between devices: 174 us -> 60.5 us
  blocking collectives: 80.7 us -> 0 us
  starting transfers between devices: 4.04 us -> 57.9 us
  matrix products: 12.5 us -> 35.8 us
  between operations: 14.5 us -> 2.07 us
  other arithmetic: 22.3 us -> 12 us
  local copies, waits for them, and re-layouts: 8.76 us -> 15.9 us
    reduce_scatter x5 -> x0, waiting for transfers between devices: 158 us -> none  [the longest x4 128 us: per_device(): lax.psum_scatter(second_state + apply_state, 'tok', scatter_dimension=1,...]
    all_gather x5 -> x0, blocking collectives: 80.7 us -> none  [the longest x4 63.2 us: per_device(): d_grad = lax.all_gather(-d_shifted, 'tok', axis=1, tiled=True)]
    ppermute x3 -> x48, starting transfers between devices: 3.84 us -> 50.9 us  [the longest x27 23.7 us: to_block(): return lax.ppermute(array, ('block', 'tok'), pairs)]
    ppermute x3 -> x48, waiting for transfers between devices: 16.6 us -> 42 us  [the longest x27 26.9 us: to_block(): return lax.ppermute(array, ('block', 'tok'), pairs)]
    dot_general x26 -> x50, matrix products: 12.5 us -> 35.8 us  [the longest x24 19.4 us: mm_nt(): lax.dot_general(left, right, (((1,), (1,)), ((), ())), precision=HIGH, pr...]
    all_to_all x0 -> x2, waiting for transfers between devices: none -> 18.5 us  [the longest x1 16.9 us: rows_to_hidden(): parts = lax.all_to_all(parts, 'tok', 0, 0)]
    add x7 -> x17, other arithmetic: 9.12 us -> 0.67 us  [the longest x8 0.46 us: per_device(): straights.append(d_shifted + dot / new * own[part] / old)]
    all_to_all x0 -> x2, starting transfers between devices: none -> 6.98 us  [the longest x1 3.61 us: hidden_to_rows(): parts = lax.all_to_all(parts, 'tok', 0, 0)]
  transfers between devices with their start and end apart: 8 -> 50, of which waited for: 8 -> 15; matrix products, arithmetic and copies ran while one was open for 2% -> 14% of each run, Pallas kernels for 0% -> 0%
where the time goes in v1:
time: 186 us; the launch traced here: 184 us
  waiting for transfers between devices  60.5 us (33%)
  starting transfers between devices  57.9 us (31%)
  matrix products  35.8 us (19%)
  local copies, waits for them, and re-layouts  15.9 us (9%)
  other arithmetic  12 us (6%)
  between operations  2.07 us (1%)
    ppermute x27, waiting for transfers between devices, to_block(): return lax.ppermute(array, ('block', 'tok'), pairs)  26.9 us
    ppermute x27, starting transfers between devices, to_block(): return lax.ppermute(array, ('block', 'tok'), pairs)  23.7 us
    ppermute x15, starting transfers between devices, chip_shift(): lax.ppermute(array, 'tok', [(j, (j + 2 * by) % size) for j in range(size)])  23.4 us
    dot_general x24, matrix products, mm_nt(): lax.dot_general(left, right, (((1,), (1,)), ((), ())), precision=HIGH, pr...  19.4 us
    all_to_all x1, waiting for transfers between devices, rows_to_hidden(): parts = lax.all_to_all(parts, 'tok', 0, 0)  16.9 us
    dot_general x23, matrix products, mm(): lax.dot_general(left, right, (((1,), (0,)), ((), ())), precision=HIGH, pr...  15.3 us
    ppermute x15, waiting for transfers between devices, chip_shift(): lax.ppermute(array, 'tok', [(j, (j + 2 * by) % size) for j in range(size)])  13.4 us
    unnamed x23, local copies, waits for them, and re-layouts  6.76 us
  transfers between devices with their start and end apart: 50, of which 15 were waited for; matrix products, arithmetic and copies ran while one was open for 14% of the time, Pallas kernels for 0%

profile of v1, /device:TPU:0, one launch (start us, length us, event | category | flops | bytes accessed | tf_op | source)
XLA Modules:
  0.0 184.3 jit_solution(579283727620605390)
XLA Ops:
  2.3 1.8 fusion.178
  4.1 3.1 %collective-permute-start.4 = (f32[2,128,256]{2,1,0:T(8,128)}, f32[2,128,256]{2,1,0:T(8,128)}, u32[]{:S(2)}, u32[]{:S(2)}) collective-permute-start(f32[2,128,256]{2,1,0:T(8,128)} %get-tuple-element.35), channel_id=1, source_target_pairs={{0,2},{1,3},{2,4},{3,5},{4,6},{5,7},{6,0},{7,1},{8,10},{9,11},{10,... | collective-permute-start | bytes 786440 | tf_op jit(solution)/shard_map/ppermute | solution.py:37
  7.1 2.6 %collective-permute-start.5 = (f32[2,128,256]{2,1,0:T(8,128)}, f32[2,128,256]{2,1,0:T(8,128)}, u32[]{:S(2)}, u32[]{:S(2)}) collective-permute-start(f32[2,128,256]{2,1,0:T(8,128)} %get-tuple-element.35), channel_id=1, source_target_pairs={{0,4},{1,5},{2,6},{3,7},{4,0},{5,1},{6,2},{7,3},{8,12},{9,13},{10,... | collective-permute-start | bytes 786440 | tf_op jit(solution)/shard_map/ppermute | solution.py:37
  9.7 1.3 collective-permute-start.6
  14.2 3.4 %all-to-all-start = ((f32[8,1,4096]{2,1,0:T(1,128)}), f32[8,1,4096]{2,1,0:T(1,128)S(1)}, u32[]{:S(2)}, u32[]{:S(2)}) async-start(f32[8,1,4096]{2,1,0:T(1,128)} %reshape.456), calls=%async_computation | async-start | bytes 262144 | tf_op jit(solution)/shard_map/all_to_all | solution.py:80
  18.5 16.9 %all-to-all-done = f32[8,1,4096]{2,1,0:T(1,128)S(1)} async-done(((f32[8,1,4096]{2,1,0:T(1,128)}), f32[8,1,4096]{2,1,0:T(1,128)S(1)}, u32[]{:S(2)}, u32[]{:S(2)}) %all-to-all-start) | async-done | bytes 131104 | tf_op jit(solution)/shard_map/all_to_all | solution.py:80
  37.8 2.2 %pad_maximum_fusion = f32[4,2,128,256]{3,2,1,0:T(8,128)} fusion(f32[1,2,128,256]{3,2,1,0:T(8,128)} %bitcast.19, f32[1,2,128,256]{3,2,1,0:T(8,128)} %bitcast.18, f32[1,2,128,256]{3,2,1,0:T(8,128)} %bitcast.17, f32[1,2,128,256]{3,2,1,0:T(8,128)} %get-tuple-element.34), kind=kLoop, calls=%fused_computation.28 | loop fusion | flops 786432 | bytes 2097152 | tf_op jit(solution)/shard_map/stack | solution.py:49
  45.0 1.3 constant_dynamic-update-slice_fusion.5
  51.8 2.0 %collective-permute-start.1 = (f32[3,32,256]{2,1,0:T(8,128)S(1)}, f32[3,32,256]{2,1,0:T(8,128)S(1)}, u32[]{:S(2)}, u32[]{:S(2)}) collective-permute-start(f32[3,32,256]{2,1,0:T(8,128)S(1)} %get-tuple-element.51), channel_id=1, source_target_pairs={{0,4},{1,5},{2,6},{3,7},{4,0},{5,1},{6,2},{7,3},{8,12},{9,13},{10,... | collective-permute-start | bytes 294920 | tf_op jit(solution)/shard_map/ppermute | solution.py:37
  56.3 3.6 %collective-permute-start.11 = (f32[6,256]{1,0:T(8,128)S(1)}, f32[6,256]{1,0:T(8,128)S(1)}, u32[]{:S(2)}, u32[]{:S(2)}) collective-permute-start(f32[6,256]{1,0:T(8,128)S(1)} %fusion.162), channel_id=1, source_target_pairs={{0,6},{1,7},{2,0},{3,1},{4,2},{5,3},{6,4},{7,5},{8,14},{9,15},{10,... | collective-permute-start | bytes 18440 | tf_op jit(solution)/shard_map/ppermute | solution.py:37
  60.0 2.5 %collective-permute-done.10 = f32[6,256]{1,0:T(8,128)S(1)} collective-permute-done((f32[6,256]{1,0:T(8,128)S(1)}, f32[6,256]{1,0:T(8,128)S(1)}, u32[]{:S(2)}, u32[]{:S(2)}) %collective-permute-start.10) | collective-permute-done | bytes 6176 | tf_op jit(solution)/shard_map/ppermute | solution.py:37
  62.5 1.6 collective-permute-start.2
  64.0 1.4 collective-permute-done.9
  67.3 1.7 collective-permute-done.3
  72.7 3.4 %collective-permute-start.17 = (f32[2,32,256]{2,1,0:T(8,128)S(1)}, f32[2,32,256]{2,1,0:T(8,128)S(1)}, u32[]{:S(2)}, u32[]{:S(2)}) collective-permute-start(f32[2,32,256]{2,1,0:T(8,128)S(1)} %get-tuple-element.48), channel_id=1, source_target_pairs={{0,8},{8,16},{16,24},{1,9},{9,17},{17,25},{2,10},{10,18},{18,26},{... | collective-permute-start | bytes 196616 | tf_op jit(solution)/shard_map/ppermute | solution.py:100
  77.6 3.4 %collective-permute-start.13 = (f32[3,32,256]{2,1,0:T(8,128)S(1)}, f32[3,32,256]{2,1,0:T(8,128)S(1)}, u32[]{:S(2)}, u32[]{:S(2)}) collective-permute-start(f32[3,32,256]{2,1,0:T(8,128)S(1)} %get-tuple-element.31), channel_id=1, source_target_pairs={{0,6},{1,7},{2,0},{3,1},{4,2},{5,3},{6,4},{7,5},{8,14},{9,15},{10,... | collective-permute-start | bytes 294920 | tf_op jit(solution)/shard_map/ppermute | solution.py:37
  82.3 1.9 %collective-permute-done.13 = f32[3,32,256]{2,1,0:T(8,128)S(1)} collective-permute-done((f32[3,32,256]{2,1,0:T(8,128)S(1)}, f32[3,32,256]{2,1,0:T(8,128)S(1)}, u32[]{:S(2)}, u32[]{:S(2)}) %collective-permute-start.13) | collective-permute-done | bytes 98336 | tf_op jit(solution)/shard_map/ppermute | solution.py:37
  84.2 6.0 %collective-permute-done.14 = f32[3,32,256]{2,1,0:T(8,128)S(1)} collective-permute-done((f32[3,32,256]{2,1,0:T(8,128)S(1)}, f32[3,32,256]{2,1,0:T(8,128)S(1)}, u32[]{:S(2)}, u32[]{:S(2)}) %collective-permute-start.14) | collective-permute-done | bytes 98336 | tf_op jit(solution)/shard_map/ppermute | solution.py:37
  115.9 1.3 collective-permute-start.36
  117.2 1.3 collective-permute-start.37
  118.5 1.3 collective-permute-start.38
  120.2 1.3 collective-permute-start.39
  121.5 1.3 collective-permute-start.40
  122.8 20.3 %collective-permute-done.36 = f32[2,256]{1,0:T(2,128)S(1)} collective-permute-done((f32[2,256]{1,0:T(2,128)S(1)}, f32[2,256]{1,0:T(2,128)S(1)}, u32[]{:S(2)}, u32[]{:S(2)}) %collective-permute-start.36) | collective-permute-done | bytes 2080 | tf_op jit(solution)/shard_map/ppermute | solution.py:95
  144.4 1.3 collective-permute-start.42
  148.1 1.3 collective-permute-start.35
  149.4 1.7 collective-permute-done.42
  151.3 3.9 %collective-permute-done.35 = f32[3,32,256]{2,1,0:T(8,128)S(1)} collective-permute-done((f32[3,32,256]{2,1,0:T(8,128)S(1)}, f32[3,32,256]{2,1,0:T(8,128)S(1)}, u32[]{:S(2)}, u32[]{:S(2)}) %collective-permute-start.35) | collective-permute-done | bytes 98336 | tf_op jit(solution)/shard_map/ppermute | solution.py:95
  162.0 1.3 collective-permute-start.45
  163.4 2.0 %collective-permute-start.46 = (f32[3,32,256]{2,1,0:T(8,128)S(1)}, f32[3,32,256]{2,1,0:T(8,128)}, u32[]{:S(2)}, u32[]{:S(2)}) collective-permute-start(f32[3,32,256]{2,1,0:T(8,128)S(1)} %get-tuple-element.47), channel_id=1, source_target_pairs={{0,6},{1,7},{2,0},{3,1},{4,2},{5,3},{6,4},{7,5},{8,14},{9,15},{10,... | collective-permute-start | bytes 294920 | tf_op jit(solution)/shard_map/ppermute | solution.py:37
  166.3 3.6 %all-to-all-start.1 = ((f32[8,1,2048]{2,1,0:T(1,128)}), f32[8,1,2048]{2,1,0:T(1,128)S(1)}, u32[]{:S(2)}, u32[]{:S(2)}) async-start(f32[8,1,2048]{2,1,0:T(1,128)} %reshape.458), calls=%async_computation.1 | async-start | bytes 131072 | tf_op jit(solution)/shard_map/all_to_all | solution.py:88
  173.9 1.6 all-to-all-done.1
  (231 shorter events, 78.7 us)
Async XLA Ops:
  4.1 33.7 %collective-permute-start.4 = (f32[2,128,256]{2,1,0:T(8,128)}, f32[2,128,256]{2,1,0:T(8,128)}, u32[]{:S(2)}, u32[]{:S(2)}) collective-permute-start(f32[2,128,256]{2,1,0:T(8,128)} %get-tuple-element.35), channel_id=1, source_target_pairs={{0,2},{1,3},{2,4},{3,5},{4,6},{5,7},{6,0},{7,1},{8,10},{9,11},{10,... | collective-permute-start | bytes 786440 | tf_op jit(solution)/shard_map/ppermute | solution.py:37
  7.1 30.7 %collective-permute-start.5 = (f32[2,128,256]{2,1,0:T(8,128)}, f32[2,128,256]{2,1,0:T(8,128)}, u32[]{:S(2)}, u32[]{:S(2)}) collective-permute-start(f32[2,128,256]{2,1,0:T(8,128)} %get-tuple-element.35), channel_id=1, source_target_pairs={{0,4},{1,5},{2,6},{3,7},{4,0},{5,1},{6,2},{7,3},{8,12},{9,13},{10,... | collective-permute-start | bytes 786440 | tf_op jit(solution)/shard_map/ppermute | solution.py:37
  9.7 28.1 %collective-permute-start.6 = (f32[2,128,256]{2,1,0:T(8,128)}, f32[2,128,256]{2,1,0:T(8,128)}, u32[]{:S(2)}, u32[]{:S(2)}) collective-permute-start(f32[2,128,256]{2,1,0:T(8,128)} %get-tuple-element.35), channel_id=1, source_target_pairs={{0,6},{1,7},{2,0},{3,1},{4,2},{5,3},{6,4},{7,5},{8,14},{9,15},{10,... | collective-permute-start | bytes 786440 | tf_op jit(solution)/shard_map/ppermute | solution.py:37
  14.2 21.2 %all-to-all-start = ((f32[8,1,4096]{2,1,0:T(1,128)}), f32[8,1,4096]{2,1,0:T(1,128)S(1)}, u32[]{:S(2)}, u32[]{:S(2)}) async-start(f32[8,1,4096]{2,1,0:T(1,128)} %reshape.456), calls=%async_computation | async-start | bytes 262144 | tf_op jit(solution)/shard_map/all_to_all | solution.py:80
  40.1 4.9 %collective-permute-start.7 = (f32[4,2,128,256]{3,2,1,0:T(8,128)}, f32[4,2,128,256]{3,2,1,0:T(8,128)}, u32[]{:S(2)}, u32[]{:S(2)}) collective-permute-start(f32[4,2,128,256]{3,2,1,0:T(8,128)} %pad_maximum_fusion), channel_id=1, source_target_pairs={{0,1},{1,0},{2,3},{3,2},{4,5},{5,4},{6,7},{7,6},{8,9},{9,8},{10,11... | collective-permute-start | bytes 3145736 | tf_op jit(solution)/shard_map/ppermute | solution.py:42
  51.6 14.9 %collective-permute-start = (f32[3,32,256]{2,1,0:T(8,128)S(1)}, f32[3,32,256]{2,1,0:T(8,128)S(1)}, u32[]{:S(2)}, u32[]{:S(2)}) collective-permute-start(f32[3,32,256]{2,1,0:T(8,128)S(1)} %get-tuple-element.51), channel_id=1, source_target_pairs={{0,2},{1,3},{2,4},{3,5},{4,6},{5,7},{6,0},{7,1},{8,10},{9,11},{10,... | collective-permute-start | bytes 294920 | tf_op jit(solution)/shard_map/ppermute | solution.py:37
  51.8 14.8 %collective-permute-start.1 = (f32[3,32,256]{2,1,0:T(8,128)S(1)}, f32[3,32,256]{2,1,0:T(8,128)S(1)}, u32[]{:S(2)}, u32[]{:S(2)}) collective-permute-start(f32[3,32,256]{2,1,0:T(8,128)S(1)} %get-tuple-element.51), channel_id=1, source_target_pairs={{0,4},{1,5},{2,6},{3,7},{4,0},{5,1},{6,2},{7,3},{8,12},{9,13},{10,... | collective-permute-start | bytes 294920 | tf_op jit(solution)/shard_map/ppermute | solution.py:37
  55.2 7.3 %collective-permute-start.10 = (f32[6,256]{1,0:T(8,128)S(1)}, f32[6,256]{1,0:T(8,128)S(1)}, u32[]{:S(2)}, u32[]{:S(2)}) collective-permute-start(f32[6,256]{1,0:T(8,128)S(1)} %fusion.162), channel_id=1, source_target_pairs={{0,4},{1,5},{2,6},{3,7},{4,0},{5,1},{6,2},{7,3},{8,12},{9,13},{10,... | collective-permute-start | bytes 18440 | tf_op jit(solution)/shard_map/ppermute | solution.py:37
  56.3 7.7 %collective-permute-start.11 = (f32[6,256]{1,0:T(8,128)S(1)}, f32[6,256]{1,0:T(8,128)S(1)}, u32[]{:S(2)}, u32[]{:S(2)}) collective-permute-start(f32[6,256]{1,0:T(8,128)S(1)} %fusion.162), channel_id=1, source_target_pairs={{0,6},{1,7},{2,0},{3,1},{4,2},{5,3},{6,4},{7,5},{8,14},{9,15},{10,... | collective-permute-start | bytes 18440 | tf_op jit(solution)/shard_map/ppermute | solution.py:37
  59.9 5.5 %collective-permute-start.9 = (f32[6,256]{1,0:T(8,128)S(1)}, f32[6,256]{1,0:T(8,128)S(1)}, u32[]{:S(2)}, u32[]{:S(2)}) collective-permute-start(f32[6,256]{1,0:T(8,128)S(1)} %fusion.162), channel_id=1, source_target_pairs={{0,2},{1,3},{2,4},{3,5},{4,6},{5,7},{6,0},{7,1},{8,10},{9,11},{10,... | collective-permute-start | bytes 18440 | tf_op jit(solution)/shard_map/ppermute | solution.py:37
  62.5 4.6 %collective-permute-start.2 = (f32[3,32,256]{2,1,0:T(8,128)S(1)}, f32[3,32,256]{2,1,0:T(8,128)S(1)}, u32[]{:S(2)}, u32[]{:S(2)}) collective-permute-start(f32[3,32,256]{2,1,0:T(8,128)S(1)} %get-tuple-element.51), channel_id=1, source_target_pairs={{0,6},{1,7},{2,0},{3,1},{4,2},{5,3},{6,4},{7,5},{8,14},{9,15},{10,... | collective-permute-start | bytes 294920 | tf_op jit(solution)/shard_map/ppermute | solution.py:37
  71.5 6.0 %collective-permute-start.12 = (f32[4,3,32,256]{3,2,1,0:T(8,128)S(1)}, f32[4,3,32,256]{3,2,1,0:T(8,128)S(1)}, u32[]{:S(2)}, u32[]{:S(2)}) collective-permute-start(f32[4,3,32,256]{3,2,1,0:T(8,128)S(1)} %slice.279), channel_id=1, source_target_pairs={{0,1},{1,0},{2,3},{3,2},{4,5},{5,4},{6,7},{7,6},{8,9},{9,8},{10,11... | collective-permute-start | bytes 1179656 | tf_op jit(solution)/shard_map/ppermute | solution.py:42
  72.7 17.5 %collective-permute-start.17 = (f32[2,32,256]{2,1,0:T(8,128)S(1)}, f32[2,32,256]{2,1,0:T(8,128)S(1)}, u32[]{:S(2)}, u32[]{:S(2)}) collective-permute-start(f32[2,32,256]{2,1,0:T(8,128)S(1)} %get-tuple-element.48), channel_id=1, source_target_pairs={{0,8},{8,16},{16,24},{1,9},{9,17},{17,25},{2,10},{10,18},{18,26},{... | collective-permute-start | bytes 196616 | tf_op jit(solution)/shard_map/ppermute | solution.py:100
  77.6 6.7 %collective-permute-start.13 = (f32[3,32,256]{2,1,0:T(8,128)S(1)}, f32[3,32,256]{2,1,0:T(8,128)S(1)}, u32[]{:S(2)}, u32[]{:S(2)}) collective-permute-start(f32[3,32,256]{2,1,0:T(8,128)S(1)} %get-tuple-element.31), channel_id=1, source_target_pairs={{0,6},{1,7},{2,0},{3,1},{4,2},{5,3},{6,4},{7,5},{8,14},{9,15},{10,... | collective-permute-start | bytes 294920 | tf_op jit(solution)/shard_map/ppermute | solution.py:37
  81.0 9.2 %collective-permute-start.14 = (f32[3,32,256]{2,1,0:T(8,128)S(1)}, f32[3,32,256]{2,1,0:T(8,128)S(1)}, u32[]{:S(2)}, u32[]{:S(2)}) collective-permute-start(f32[3,32,256]{2,1,0:T(8,128)S(1)} %get-tuple-element.33), channel_id=1, source_target_pairs={{0,4},{1,5},{2,6},{3,7},{4,0},{5,1},{6,2},{7,3},{8,12},{9,13},{10,... | collective-permute-start | bytes 294920 | tf_op jit(solution)/shard_map/ppermute | solution.py:37
  81.0 9.2 %collective-permute-start.15 = (f32[3,32,256]{2,1,0:T(8,128)S(1)}, f32[3,32,256]{2,1,0:T(8,128)S(1)}, u32[]{:S(2)}, u32[]{:S(2)}) collective-permute-start(f32[3,32,256]{2,1,0:T(8,128)S(1)} %get-tuple-element.32), channel_id=1, source_target_pairs={{0,2},{1,3},{2,4},{3,5},{4,6},{5,7},{6,0},{7,1},{8,10},{9,11},{10,... | collective-permute-start | bytes 294920 | tf_op jit(solution)/shard_map/ppermute | solution.py:37
  103.1 4.4 %collective-permute-start.28 = (f32[2,256]{1,0:T(2,128)S(1)}, f32[2,256]{1,0:T(2,128)S(1)}, u32[]{:S(2)}, u32[]{:S(2)}) collective-permute-start(f32[2,256]{1,0:T(2,128)S(1)} %fusion.119), channel_id=1, source_target_pairs={{16,9},{17,10},{18,11},{19,12},{20,13},{21,14},{22,15},{23,8}} | collective-permute-start | bytes 6152 | tf_op jit(solution)/shard_map/ppermute | solution.py:95
  103.8 4.4 %collective-permute-start.29 = (f32[2,256]{1,0:T(2,128)S(1)}, f32[2,256]{1,0:T(2,128)S(1)}, u32[]{:S(2)}, u32[]{:S(2)}) collective-permute-start(f32[2,256]{1,0:T(2,128)S(1)} %fusion.119), channel_id=1, source_target_pairs={{16,10},{17,11},{18,12},{19,13},{20,14},{21,15},{22,8},{23,9}} | collective-permute-start | bytes 6152 | tf_op jit(solution)/shard_map/ppermute | solution.py:95
  115.9 27.2 %collective-permute-start.36 = (f32[2,256]{1,0:T(2,128)S(1)}, f32[2,256]{1,0:T(2,128)S(1)}, u32[]{:S(2)}, u32[]{:S(2)}) collective-permute-start(f32[2,256]{1,0:T(2,128)S(1)} %fusion.117), channel_id=1, source_target_pairs={{8,0},{9,1},{10,2},{11,3},{12,4},{13,5},{14,6},{15,7}} | collective-permute-start | bytes 6152 | tf_op jit(solution)/shard_map/ppermute | solution.py:95
  117.2 27.2 %collective-permute-start.37 = (f32[2,256]{1,0:T(2,128)S(1)}, f32[2,256]{1,0:T(2,128)S(1)}, u32[]{:S(2)}, u32[]{:S(2)}) collective-permute-start(f32[2,256]{1,0:T(2,128)S(1)} %fusion.117), channel_id=1, source_target_pairs={{8,1},{9,2},{10,3},{11,4},{12,5},{13,6},{14,7},{15,0}} | collective-permute-start | bytes 6152 | tf_op jit(solution)/shard_map/ppermute | solution.py:95
  118.5 27.9 %collective-permute-start.38 = (f32[2,256]{1,0:T(2,128)S(1)}, f32[2,256]{1,0:T(2,128)S(1)}, u32[]{:S(2)}, u32[]{:S(2)}) collective-permute-start(f32[2,256]{1,0:T(2,128)S(1)} %fusion.117), channel_id=1, source_target_pairs={{8,2},{9,3},{10,4},{11,5},{12,6},{13,7},{14,0},{15,1}} | collective-permute-start | bytes 6152 | tf_op jit(solution)/shard_map/ppermute | solution.py:95
  120.2 27.9 %collective-permute-start.39 = (f32[2,256]{1,0:T(2,128)S(1)}, f32[2,256]{1,0:T(2,128)S(1)}, u32[]{:S(2)}, u32[]{:S(2)}) collective-permute-start(f32[2,256]{1,0:T(2,128)S(1)} %fusion.117), channel_id=1, source_target_pairs={{8,3},{9,4},{10,5},{11,6},{12,7},{13,0},{14,1},{15,2}} | collective-permute-start | bytes 6152 | tf_op jit(solution)/shard_map/ppermute | solution.py:95
  121.5 27.9 %collective-permute-start.40 = (f32[2,256]{1,0:T(2,128)S(1)}, f32[2,256]{1,0:T(2,128)S(1)}, u32[]{:S(2)}, u32[]{:S(2)}) collective-permute-start(f32[2,256]{1,0:T(2,128)S(1)} %fusion.117), channel_id=1, source_target_pairs={{8,4},{9,5},{10,6},{11,7},{12,0},{13,1},{14,2},{15,3}} | collective-permute-start | bytes 6152 | tf_op jit(solution)/shard_map/ppermute | solution.py:95
  143.1 6.3 %collective-permute-start.41 = (f32[2,256]{1,0:T(2,128)S(1)}, f32[2,256]{1,0:T(2,128)S(1)}, u32[]{:S(2)}, u32[]{:S(2)}) collective-permute-start(f32[2,256]{1,0:T(2,128)S(1)} %fusion.117), channel_id=1, source_target_pairs={{8,5},{9,6},{10,7},{11,0},{12,1},{13,2},{14,3},{15,4}} | collective-permute-start | bytes 6152 | tf_op jit(solution)/shard_map/ppermute | solution.py:95
  144.4 6.7 %collective-permute-start.42 = (f32[2,256]{1,0:T(2,128)S(1)}, f32[2,256]{1,0:T(2,128)S(1)}, u32[]{:S(2)}, u32[]{:S(2)}) collective-permute-start(f32[2,256]{1,0:T(2,128)S(1)} %fusion.117), channel_id=1, source_target_pairs={{8,6},{9,7},{10,0},{11,1},{12,2},{13,3},{14,4},{15,5}} | collective-permute-start | bytes 6152 | tf_op jit(solution)/shard_map/ppermute | solution.py:95
  146.4 4.9 %collective-permute-start.43 = (f32[2,256]{1,0:T(2,128)S(1)}, f32[2,256]{1,0:T(2,128)S(1)}, u32[]{:S(2)}, u32[]{:S(2)}) collective-permute-start(f32[2,256]{1,0:T(2,128)S(1)} %fusion.117), channel_id=1, source_target_pairs={{8,7},{9,0},{10,1},{11,2},{12,3},{13,4},{14,5},{15,6}} | collective-permute-start | bytes 6152 | tf_op jit(solution)/shard_map/ppermute | solution.py:95
  148.1 7.2 %collective-permute-start.35 = (f32[3,32,256]{2,1,0:T(8,128)S(1)}, f32[3,32,256]{2,1,0:T(8,128)S(1)}, u32[]{:S(2)}, u32[]{:S(2)}) collective-permute-start(f32[3,32,256]{2,1,0:T(8,128)S(1)} %fusion.109), channel_id=1, source_target_pairs={{8,0},{9,1},{10,2},{11,3},{12,4},{13,5},{14,6},{15,7}} | collective-permute-start | bytes 294920 | tf_op jit(solution)/shard_map/ppermute | solution.py:95
  161.5 8.5 %collective-permute-start.44 = (f32[3,32,256]{2,1,0:T(8,128)S(1)}, f32[3,32,256]{2,1,0:T(8,128)S(1)}, u32[]{:S(2)}, u32[]{:S(2)}) collective-permute-start(f32[3,32,256]{2,1,0:T(8,128)S(1)} %get-tuple-element.47), channel_id=1, source_target_pairs={{0,2},{1,3},{2,4},{3,5},{4,6},{5,7},{6,0},{7,1},{8,10},{9,11},{10,... | collective-permute-start | bytes 294920 | tf_op jit(solution)/shard_map/ppermute | solution.py:37
  162.0 8.9 %collective-permute-start.45 = (f32[3,32,256]{2,1,0:T(8,128)S(1)}, f32[3,32,256]{2,1,0:T(8,128)}, u32[]{:S(2)}, u32[]{:S(2)}) collective-permute-start(f32[3,32,256]{2,1,0:T(8,128)S(1)} %get-tuple-element.47), channel_id=1, source_target_pairs={{0,4},{1,5},{2,6},{3,7},{4,0},{5,1},{6,2},{7,3},{8,12},{9,13},{10,... | collective-permute-start | bytes 294920 | tf_op jit(solution)/shard_map/ppermute | solution.py:37
  163.4 7.6 %collective-permute-start.46 = (f32[3,32,256]{2,1,0:T(8,128)S(1)}, f32[3,32,256]{2,1,0:T(8,128)}, u32[]{:S(2)}, u32[]{:S(2)}) collective-permute-start(f32[3,32,256]{2,1,0:T(8,128)S(1)} %get-tuple-element.47), channel_id=1, source_target_pairs={{0,6},{1,7},{2,0},{3,1},{4,2},{5,3},{6,4},{7,5},{8,14},{9,15},{10,... | collective-permute-start | bytes 294920 | tf_op jit(solution)/shard_map/ppermute | solution.py:37
  166.3 9.2 %all-to-all-start.1 = ((f32[8,1,2048]{2,1,0:T(1,128)}), f32[8,1,2048]{2,1,0:T(1,128)S(1)}, u32[]{:S(2)}, u32[]{:S(2)}) async-start(f32[8,1,2048]{2,1,0:T(1,128)} %reshape.458), calls=%async_computation.1 | async-start | bytes 131072 | tf_op jit(solution)/shard_map/all_to_all | solution.py:88
  172.0 5.4 %collective-permute-start.47 = (f32[4,3,32,256]{3,2,1,0:T(8,128)S(1)}, f32[4,3,32,256]{3,2,1,0:T(8,128)}, u32[]{:S(2)}, u32[]{:S(2)}) collective-permute-start(f32[4,3,32,256]{3,2,1,0:T(8,128)S(1)} %pad_maximum_fusion.2), channel_id=1, source_target_pairs={{0,1},{1,0},{2,3},{3,2},{4,5},{5,4},{6,7},{7,6},{8,9},{9,8},{10,11... | collective-permute-start | bytes 1179656 | tf_op jit(solution)/shard_map/ppermute | solution.py:42
  (23 other events, 156.8 us)

commit v2 on v1

--- a/solution.py
+++ b/solution.py
@@ -1,6 +1,8 @@
 import jax
 import jax.numpy as jnp
 from jax import lax
+from jax.experimental import pallas as pl
+from jax.experimental.pallas import tpu as pltpu
 from jax.sharding import PartitionSpec as P
 
 EPS = 1e-06
@@ -151,7 +153,7 @@
     return jnp.sum(array[:2], axis=1)
 
 
-def per_device(queries, keys, values, rates, states, out_cot, final_cot):
+def per_device_general(queries, keys, values, rates, states, out_cot, final_cot):
     groups, size = lax.axis_size("block"), lax.axis_size("tok")
     position = lax.axis_index("block")
     own_rows = states[0]
@@ -206,6 +208,358 @@
     return (d_queries, d_keys, d_values, d_rates, d_rows[None])
 
 
+def halves(array):
+    upper = array.astype(jnp.bfloat16)
+    return upper, (array - upper.astype(jnp.float32)).astype(jnp.bfloat16)
+
+
+def product(left, right, contract):
+    def one(a, b):
+        return lax.dot_general(a, b, (((1,), (contract,)), ((), ())), preferred_element_type=jnp.float32)
+
+    return one(left[0], right[0]) + (one(left[0], right[1]) + one(left[1], right[0]))
+
+
+def nn(left, right):
+    return product(left, right, 0)
+
+
+def nt(left, right):
+    return product(left, right, 1)
+
+
+def kernel_call(body, name, outs, *operands, flag=None):
+    specs = [pl.BlockSpec(memory_space=pltpu.VMEM) for _ in operands]
+    if flag is not None:
+        specs = [pl.BlockSpec(memory_space=pltpu.SMEM)] + specs
+        operands = (flag,) + operands
+    return pl.pallas_call(
+        body,
+        name=name,
+        in_specs=specs,
+        out_specs=[pl.BlockSpec(memory_space=pltpu.VMEM) for _ in outs],
+        out_shape=[jax.ShapeDtypeStruct(shape, dtype) for shape, dtype in outs],
+    )(*operands)
+
+
+def f32(*shape):
+    return shape, jnp.float32
+
+
+def bf16(*shape):
+    return shape, jnp.bfloat16
+
+
+def column(row, width):
+    block = jnp.broadcast_to(row, (128, row.shape[1])).T
+    return jnp.concatenate([block] * (width // 128), axis=1)
+
+
+def pack_body(values, rates, rows, final, scaled, packed):
+    scaled[...] = -column(rates[...], values.shape[1]) * values[...]
+    depth, width = rows.shape[1:]
+    count = packed.shape[0] // depth
+    span = width // count
+    for peer in range(count):
+        cut = slice(peer * span, (peer + 1) * span)
+        parts = [rows[0, :, cut], rows[1, :, cut], final[0, :, cut], final[1, :, cut]]
+        packed[peer * depth : (peer + 1) * depth, :] = jnp.concatenate(parts, axis=1)
+
+
+def unpack_body(flag, arrived, rows, final, own, last):
+    span = own.shape[1]
+    turned = arrived[...].T
+    own[0] = turned[:span]
+    own[1] = turned[span : 2 * span]
+    own[2] = rows[2]
+    keep = jnp.where(flag[0] != 0, 1.0, 0.0)
+    last[0] = turned[2 * span : 3 * span] * keep
+    last[1] = turned[3 * span :] * keep
+    last[2] = final[2] * keep
+
+
+CHUNK = 256
+
+
+def forward_body(own, last, *refs):
+    pieces = (len(refs) - 7) // 2
+    keys, scaled = refs[:pieces], refs[pieces : 2 * pieces]
+    key_high, key_low, scaled_high, scaled_low, kept, shifted, sums = refs[2 * pieces :]
+    depth = keys[0].shape[0]
+    for index in range(pieces):
+        cut = slice(index * depth, (index + 1) * depth)
+        key_high[cut, :], key_low[cut, :] = halves(keys[index][...])
+        scaled_high[cut, :], scaled_low[cut, :] = halves(scaled[index][...])
+    span = own.shape[1]
+    pair = halves(jnp.concatenate([own[0], own[1]]))
+    second = halves(own[2])
+    grad_pair, grad_second = 0.0, 0.0
+    for start in range(0, pieces * depth, CHUNK):
+        cut = slice(start, start + CHUNK)
+        key_cut = key_high[cut, :], key_low[cut, :]
+        scaled_cut = scaled_high[cut, :], scaled_low[cut, :]
+        both = nt(pair, key_cut)
+        d_mixed = nt(second, scaled_cut)
+        first, gate = both[:span], both[span:]
+        value, d_one, d_two = silu_parts(first)
+        for place, array in enumerate((gate, value, d_one, d_two, d_mixed)):
+            kept[place, :, cut] = array
+        d_pair = jnp.concatenate([d_mixed * gate * d_one, d_mixed * value])
+        grad_pair += nn(halves(d_pair), key_cut)
+        grad_second += nn(halves(value * gate), scaled_cut)
+    moved = own[0] - grad_pair[:span], own[1] - grad_pair[span:], own[2] - grad_second
+    rows = []
+    for left, right in ((own, own), (moved, moved), (last, moved)):
+        rows += [jnp.sum(left[m] * right[m], axis=0, keepdims=True) for m in range(2)]
+    sums[...] = jnp.concatenate(rows + [jnp.zeros((2, own.shape[2]), jnp.float32)])
+    for m in range(3):
+        shifted[m] = moved[m]
+
+
+def state_terms(own, shifted, last, sums, inners, arrived):
+    span = own.shape[1]
+    total = sums[0][...] + sums[1][...]
+    inner = total[4:6]
+    for array in inners:
+        inner = inner + array[0:2]
+    cots, straights = [], []
+    for m in range(3):
+        incoming = last[m]
+        for array in arrived:
+            incoming = incoming + array[m * span : (m + 1) * span, :]
+        if m < 2:
+            dot, old, new = inner[m : m + 1], jnp.sqrt(total[m : m + 1] + EPS), jnp.sqrt(total[m + 2 : m + 3] + EPS)
+        else:
+            dot = jnp.sum(incoming * shifted[m], axis=-1, keepdims=True)
+            old = jnp.sqrt(jnp.sum(own[m] * own[m], axis=-1, keepdims=True) + EPS)
+            new = jnp.sqrt(jnp.sum(shifted[m] * shifted[m], axis=-1, keepdims=True) + EPS)
+        d_shifted = old / new * incoming - old * dot / (new * new * new) * shifted[m]
+        cots.append(-d_shifted)
+        straights.append(d_shifted + dot / new * own[m] / old)
+    return cots, straights
+
+
+def terms_body(count, *refs):
+    own, shifted, last, sum_a, sum_b = refs[:5]
+    inners, arrived = refs[5 : 5 + 2 * count], refs[5 + 2 * count : 5 + 3 * count]
+    cot = refs[-1]
+    cots, _ = state_terms(own, shifted, last, (sum_a, sum_b), inners, arrived)
+    for m in range(3):
+        cot[m] = cots[m]
+
+
+def section_body(count, final, flag, *refs):
+    own, shifted, last, sum_a, sum_b, earlier = refs[:6]
+    key_high, key_low, scaled_high, scaled_low, kept = refs[6:11]
+    refs = refs[11:]
+    inners, arrived, refs = refs[: 2 * count], refs[2 * count : 3 * count], refs[3 * count :]
+    applied, outs = refs[:-2], refs[-2:]
+    span = own.shape[1]
+
+    @pl.when(flag[0] != 0)
+    def _():
+        cots, straights = state_terms(own, shifted, last, (sum_a, sum_b), inners, arrived)
+        pair = halves(jnp.concatenate(cots[:2]))
+        second = halves(cots[2])
+        d_pair, d_second = 0.0, 0.0
+        for start in range(0, key_high.shape[0], CHUNK):
+            cut = slice(start, start + CHUNK)
+            key_cut = key_high[cut, :], key_low[cut, :]
+            scaled_cut = scaled_high[cut, :], scaled_low[cut, :]
+            gate, value, d_one, d_two, d_mixed = [kept[place, :, cut] for place in range(5)]
+            both = nt(pair, key_cut)
+            p_mixed = nt(second, scaled_cut)
+            t_first, t_gate = both[:span], both[span:]
+            lift = d_one * t_first
+            t_mixed = lift * gate + value * t_gate
+            c_gate = p_mixed * value + d_mixed * lift
+            c_first = p_mixed * gate * d_one + d_mixed * (d_two * t_first * gate + d_one * t_gate)
+            d_pair += nn(halves(jnp.concatenate([c_first, c_gate])), key_cut)
+            d_second += nn(halves(t_mixed), scaled_cut)
+        rows = [d_pair[:span] + straights[0], d_pair[span:] + straights[1], d_second + straights[2]]
+        for array in applied:
+            rows = [row + array[m * span : (m + 1) * span, :] for m, row in enumerate(rows)]
+        width = own.shape[2]
+        if final:
+            out_pair, out_second = outs
+            out_pair[...] = jnp.concatenate([rows[0], rows[1], jnp.zeros((128 - 2 * span, width), jnp.float32)]).T
+            out_second[...] = rows[2]
+        else:
+            payload, partial = outs
+            sums = [jnp.sum(rows[m] * earlier[m], axis=0, keepdims=True) for m in range(2)]
+            tail = jnp.concatenate(sums + [jnp.zeros((6, width), jnp.float32)])
+            partial[...] = tail
+            payload[...] = jnp.concatenate(rows + [tail])
+
+
+def load_halves(pieces, part):
+    return halves(jnp.concatenate([piece[part] for piece in pieces]))
+
+
+def query_body(queries, out_cot, *refs):
+    size = (len(refs) - 1) // 2
+    pieces, d_queries, outs = refs[:size], refs[size], refs[size + 1 :]
+    span = pieces[0].shape[1]
+    one, three, two = [load_halves(pieces, part) for part in range(3)]
+    query, cot = halves(queries[...]), halves(out_cot[...])
+    first, gate = nt(query, one), nt(query, three)
+    value, d_one, _ = silu_parts(first)
+    d_mixed = nt(cot, two)
+    d_gate = d_mixed * value
+    d_first = d_mixed * gate * d_one
+    d_queries[...] = nn(halves(d_first), one) + nn(halves(d_gate), three)
+    parts = nn(halves(d_first.T), query), nn(halves(d_gate.T), query), nn(halves((value * gate).T), cot)
+    for index, out in enumerate(outs):
+        out[...] = jnp.concatenate([part[index * span : (index + 1) * span] for part in parts])
+
+
+def token_body(keys, values, rates, arrived, second, *refs):
+    size = (len(refs) - 4) // 2
+    weights, cots = refs[:size], refs[size : 2 * size]
+    d_keys, d_values, d_rates, d_rows = refs[2 * size :]
+    width = keys.shape[1]
+    one, three, two = [load_halves(weights, part) for part in range(3)]
+    c_one, c_three, c_two = [load_halves(cots, part) for part in range(3)]
+    rate = column(rates[...], width)
+    key, scaled = halves(keys[...]), halves(-rate * values[...])
+    first, gate = nt(key, one), nt(key, three)
+    value, d_one, d_two = silu_parts(first)
+    d_mixed = nt(scaled, two)
+    t_first, t_gate, p_mixed = nt(key, c_one), nt(key, c_three), nt(scaled, c_two)
+    mixed = value * gate
+    d_gate = d_mixed * value
+    d_first = d_mixed * gate * d_one
+    lift = d_one * t_first
+    t_mixed = lift * gate + value * t_gate
+    c_gate = p_mixed * value + d_mixed * lift
+    c_first = p_mixed * gate * d_one + d_mixed * (d_two * t_first * gate + d_one * t_gate)
+    d_keys[...] = nn(halves(c_first), one) + nn(halves(c_gate), three) + nn(halves(d_first), c_one) + nn(halves(d_gate), c_three)
+    t_out = nn(halves(t_mixed), two) + nn(halves(mixed), c_two)
+    d_values[...] = -rate * t_out
+    d_rates[...] = -jnp.sum((values[...] * t_out).T, axis=0, keepdims=True)
+    depth, span = d_rows.shape[1], weights[0].shape[1]
+    for m in range(2):
+        parts = [arrived[j * depth : (j + 1) * depth, m * span : (m + 1) * span] for j in range(size)]
+        d_rows[m] = jnp.concatenate(parts, axis=1)
+    d_rows[2] = second[...]
+
+
+def gather_list(array):
+    size = lax.axis_size("tok")
+    mine = [array] + [chip_shift(array, by) for by in range(1, size // 2)]
+    return mine + [core_swap(piece) for piece in mine]
+
+
+def per_device(queries, keys, values, rates, states, out_cot, final_cot):
+    groups, size = lax.axis_size("block"), lax.axis_size("tok")
+    depth, width = keys.shape
+    span = width // size
+    rows = states.shape[2]
+    if not (direct(size) and 4 * span == 128 and depth % 128 == 0 and width % 128 == 0):
+        return per_device_general(queries, keys, values, rates, states, out_cot, final_cot)
+    tokens = depth * size
+    position = lax.axis_index("block")
+    own_rows = states[0]
+    rates_row = rates.reshape(1, depth)
+    scaled, packed = kernel_call(
+        pack_body, "pack", [f32(depth, width), f32(width, 4 * span)], values, rates_row, own_rows, final_cot
+    )
+    turned = lax.all_to_all(packed, "tok", 0, 0, tiled=True)
+    key_pieces = gather_list(keys)
+    scaled_pieces = gather_list(scaled)
+    is_last = (position == groups - 1).astype(jnp.int32).reshape(1)
+    state = f32(3, span, width)
+    own, last = kernel_call(unpack_body, "unpack", [state, state], turned, own_rows, final_cot, flag=is_last)
+    half = bf16(tokens, width)
+    *halved, kept, shifted, sums = kernel_call(
+        forward_body,
+        "forward",
+        [half, half, half, half, f32(5, span, tokens), state, f32(8, width)],
+        own,
+        last,
+        *key_pieces,
+        *scaled_pieces,
+    )
+    earlier = up_one(shifted[:2])
+    sum_a = sums
+    for by in range(1, size // 2):
+        sum_a = sum_a + chip_shift(sums, by)
+    sum_b = core_swap(sum_a)
+
+    pieces = gather_list(own)
+    piece = f32(3 * span, width)
+    d_queries, *parts = kernel_call(query_body, "query", [f32(depth, width)] + [piece] * size, queries, out_cot, *pieces)
+    near, far = parts[: size // 2], parts[size // 2 :]
+    mine = [a + core_swap(b) for a, b in zip(near, far)]
+    applied = [mine[0]] + [chip_shift(mine[by], -by) for by in range(1, size // 2)]
+
+    inners, arrived = [], []
+    common = [own, shifted, last, sum_a, sum_b]
+    for section in range(groups - 1):
+        source = groups - 1 - section
+        active = (position == source).astype(jnp.int32).reshape(1)
+
+        def body(*refs, count=section):
+            section_body(count, False, *refs)
+
+        payload, partial = kernel_call(
+            body,
+            "section",
+            [f32(3 * span + 8, width), f32(8, width)],
+            *common,
+            earlier,
+            *halved,
+            kept,
+            *inners,
+            *arrived,
+            *applied,
+            flag=active,
+        )
+        got = to_block(payload, source, source - 1)
+        inner = got[3 * span :]
+        for by in range(1, size // 2):
+            inner = inner + to_block(partial, source, source - 1, 2 * by)
+        arrived = arrived + [got]
+        inners = inners + [inner, core_swap(inner)]
+
+    def terms(*refs):
+        terms_body(groups - 1, *refs)
+
+    def body(*refs):
+        section_body(groups - 1, True, *refs)
+
+    (cot,) = kernel_call(terms, "terms", [state], *common, *inners, *arrived)
+    cot_pieces = gather_list(cot)
+    always = jnp.ones((1,), jnp.int32)
+    pair, second = kernel_call(
+        body,
+        "final",
+        [f32(width, 128), f32(span, width)],
+        *common,
+        earlier,
+        *halved,
+        kept,
+        *inners,
+        *arrived,
+        *applied,
+        flag=always,
+    )
+    turned = lax.all_to_all(pair, "tok", 0, 0, tiled=True)
+    d_keys, d_values, d_rates, d_rows = kernel_call(
+        token_body,
+        "token",
+        [f32(depth, width), f32(depth, width), f32(1, depth), f32(3, rows, width)],
+        keys,
+        values,
+        rates_row,
+        turned,
+        second,
+        *pieces,
+        *cot_pieces,
+    )
+    return (d_queries, d_keys, d_values, d_rates.reshape(depth), d_rows[None])
+
+
 def solution(mesh):
     return jax.shard_map(
         per_device,

time: 186 us -> 156 us (0.84)
  matrix products: 35.8 us -> 0 us
  Pallas kernels: 0 us -> 30.1 us
  other arithmetic: 12 us -> 0.73 us
  local copies, waits for them, and re-layouts: 15.9 us -> 6.63 us
  waiting for transfers between devices: 60.5 us -> 56.3 us
  starting transfers between devices: 57.9 us -> 60.3 us
    dot_general x50 -> x0, matrix products: 35.8 us -> none  [the longest x24 19.4 us: mm_nt(): lax.dot_general(left, right, (((1,), (1,)), ((), ())), precision=HIGH, pr...]
    pallas_call x0 -> x10, Pallas kernels: none -> 30.1 us  [kernel_call(): pl.pallas_call(body, name=name, in_specs=specs, out_specs=[pl.BlockSpec(m...]
    all_to_all x2, waiting for transfers between devices: 18.5 us -> 0.01 us  [the longest x1 0.01 us: per_device(): turned = lax.all_to_all(packed, 'tok', 0, 0, tiled=True)]
    ppermute x15 -> x18, waiting for transfers between devices: 13.4 us -> 28.7 us  [chip_shift(): lax.ppermute(array, 'tok', [(j, (j + 2 * by) % size) for j in range(size)])]
    ppermute x27 -> x12, starting transfers between devices: 23.7 us -> 10.4 us  [to_block(): return lax.ppermute(array, ('block', 'tok'), pairs)]
    ppermute x15 -> x18, starting transfers between devices: 23.4 us -> 32.4 us  [chip_shift(): lax.ppermute(array, 'tok', [(j, (j + 2 * by) % size) for j in range(size)])]
    another operation x6 -> x0, other arithmetic: 6.68 us -> none  [the longest x5 5.7 us: gather_pieces(): jnp.stack([array] + [chip_shift(array, by) for by in range(1, size // 2)])]
    slice x18 -> x1, local copies, waits for them, and re-layouts: 5.19 us -> 0.85 us  [per_device(): earlier = up_one(shifted[:2])]
  transfers between devices with their start and end apart: 50 -> 57, of which waited for: 15 -> 19; matrix products, arithmetic and copies ran while one was open for 14% -> 1% of each run, Pallas kernels for 0% -> 7%
where the time goes in v2:
time: 156 us; the launch traced here: 155 us
  starting transfers between devices  60.3 us (39%)
  waiting for transfers between devices  56.3 us (36%)
  Pallas kernels  30.1 us (19%)
  local copies, waits for them, and re-layouts  6.63 us (4%)
    ppermute x18, starting transfers between devices, chip_shift(): lax.ppermute(array, 'tok', [(j, (j + 2 * by) % size) for j in range(size)])  32.4 us
    pallas_call x10, Pallas kernels, kernel_call(): pl.pallas_call(body, name=name, in_specs=specs, out_specs=[pl.BlockSpec(m...  30.1 us
    ppermute x18, waiting for transfers between devices, chip_shift(): lax.ppermute(array, 'tok', [(j, (j + 2 * by) % size) for j in range(size)])  28.7 us
    ppermute x12, waiting for transfers between devices, to_block(): return lax.ppermute(array, ('block', 'tok'), pairs)  22.7 us
    ppermute x12, starting transfers between devices, to_block(): return lax.ppermute(array, ('block', 'tok'), pairs)  10.4 us
    all_to_all x1, starting transfers between devices, per_device(): turned = lax.all_to_all(packed, 'tok', 0, 0, tiled=True)  6.49 us
    unnamed x106, local copies, waits for them, and re-layouts  5.78 us
    ppermute x24, waiting for transfers between devices, core_swap(): return lax.ppermute(array, 'tok', [(j, j ^ 1) for j in range(size)])  4.94 us
  transfers between devices with their start and end apart: 57, of which 19 were waited for; matrix products, arithmetic and copies ran while one was open for 1% of the time, Pallas kernels for 7%

profile of v2, /device:TPU:0, one launch (start us, length us, event | category | flops | bytes accessed | tf_op | source)
XLA Modules:
  0.0 155.4 jit_solution(14461778684028984260)
XLA Ops:
  0.6 1.9 %pack.1 = (f32[128,256]{1,0:T(8,128)}, f32[256,128]{1,0:T(8,128)}) custom-call(f32[128,256]{1,0:T(8,128)} %values.3, f32[1,128]{1,0:T(1,128)} %bitcast.17, f32[3,32,256]{2,1,0:T(8,128)} %bitcast.13, f32[3,32,256]{2,1,0:T(8,128)} %final.4), custom_call_target="tpu_custom_call" | custom-call | tf_op jit(solution)/shard_map/pack/pallas_call | solution.py:236
  2.5 6.5 %all-to-all-start = ((f32[8,32,128]{2,1,0:T(8,128)}), f32[8,32,128]{2,1,0:T(8,128)S(1)}, u32[]{:S(2)}, u32[]{:S(2)}) async-start(f32[8,32,128]{2,1,0:T(8,128)} %bitcast.16), calls=%async_computation | async-start | bytes 262144 | tf_op jit(solution)/shard_map/all_to_all | solution.py:467
  9.0 2.0 %collective-permute-start.14 = (f32[128,256]{1,0:T(8,128)S(1)}, f32[128,256]{1,0:T(8,128)S(1)}, u32[]{:S(2)}, u32[]{:S(2)}) collective-permute-start(f32[128,256]{1,0:T(8,128)S(1)} %copy-done.22), channel_id=1, source_target_pairs={{0,2},{1,3},{2,4},{3,5},{4,6},{5,7},{6,0},{7,1},{8,10},{9,11},{10,... | collective-permute-start | bytes 393224 | tf_op jit(solution)/shard_map/ppermute | solution.py:39
  11.0 2.4 %collective-permute-start.15 = (f32[128,256]{1,0:T(8,128)S(1)}, f32[128,256]{1,0:T(8,128)S(1)}, u32[]{:S(2)}, u32[]{:S(2)}) collective-permute-start(f32[128,256]{1,0:T(8,128)S(1)} %copy-done.22), channel_id=1, source_target_pairs={{0,4},{1,5},{2,6},{3,7},{4,0},{5,1},{6,2},{7,3},{8,12},{9,13},{10,... | collective-permute-start | bytes 393224 | tf_op jit(solution)/shard_map/ppermute | solution.py:39
  13.4 1.5 collective-permute-start.16
  15.4 4.1 %collective-permute-done.14.refs_9_ = f32[128,256]{1,0:T(8,128)S(1)} collective-permute-done((f32[128,256]{1,0:T(8,128)S(1)}, f32[128,256]{1,0:T(8,128)S(1)}, u32[]{:S(2)}, u32[]{:S(2)}) %collective-permute-start.14) | collective-permute-done | bytes 131104 | tf_op jit(solution)/shard_map/ppermute | solution.py:39
  19.5 5.5 %collective-permute-start.8 = (f32[128,256]{1,0:T(8,128)S(1)}, f32[128,256]{1,0:T(8,128)S(1)}, u32[]{:S(2)}, u32[]{:S(2)}) collective-permute-start(f32[128,256]{1,0:T(8,128)S(1)} %copy-done.6), channel_id=1, source_target_pairs={{0,4},{1,5},{2,6},{3,7},{4,0},{5,1},{6,2},{7,3},{8,12},{9,13},{10,... | collective-permute-start | bytes 393224 | tf_op jit(solution)/shard_map/ppermute | solution.py:39
  24.9 4.8 %collective-permute-done.15.refs_10_ = f32[128,256]{1,0:T(8,128)S(1)} collective-permute-done((f32[128,256]{1,0:T(8,128)S(1)}, f32[128,256]{1,0:T(8,128)S(1)}, u32[]{:S(2)}, u32[]{:S(2)}) %collective-permute-start.15) | collective-permute-done | bytes 131104 | tf_op jit(solution)/shard_map/ppermute | solution.py:39
  30.5 1.8 %unpack.1 = (f32[3,32,256]{2,1,0:T(8,128)}, f32[3,32,256]{2,1,0:T(8,128)}) custom-call(s32[1]{0:T(128)} %bitcast.flag.refs_0_, f32[256,128]{1,0:T(8,128)} %bitcast.12, f32[3,32,256]{2,1,0:T(8,128)} %bitcast.14, f32[3,32,256]{2,1,0:T(8,128)} %final.4), custom_call_target="tpu_custom_call" | custom-call | tf_op jit(solution)/shard_map/unpack/pallas_call | solution.py:236
  32.3 3.8 %collective-permute-start = (f32[3,32,256]{2,1,0:T(8,128)}, f32[3,32,256]{2,1,0:T(8,128)S(1)}, u32[]{:S(2)}, u32[]{:S(2)}) collective-permute-start(f32[3,32,256]{2,1,0:T(8,128)} %get-tuple-element.38.refs_0_.own.refs_1_), channel_id=1, source_target_pairs={{0,2},{1,3},{2,4},{3,5},{4,6},{5,7},{6,0},{7,1},{8,10},{9,11},{10,... | collective-permute-start | bytes 294920 | tf_op jit(solution)/shard_map/ppermute | solution.py:39
  37.0 2.9 %collective-permute-start.2 = (f32[3,32,256]{2,1,0:T(8,128)}, f32[3,32,256]{2,1,0:T(8,128)S(1)}, u32[]{:S(2)}, u32[]{:S(2)}) collective-permute-start(f32[3,32,256]{2,1,0:T(8,128)} %get-tuple-element.38.refs_0_.own.refs_1_), channel_id=1, source_target_pairs={{0,6},{1,7},{2,0},{3,1},{4,2},{5,3},{6,4},{7,5},{8,14},{9,15},{10,... | collective-permute-start | bytes 294920 | tf_op jit(solution)/shard_map/ppermute | solution.py:39
  40.4 4.6 %collective-permute-done.1.refs_2_ = f32[3,32,256]{2,1,0:T(8,128)S(1)} collective-permute-done((f32[3,32,256]{2,1,0:T(8,128)}, f32[3,32,256]{2,1,0:T(8,128)S(1)}, u32[]{:S(2)}, u32[]{:S(2)}) %collective-permute-start.1) | collective-permute-done | bytes 98336 | tf_op jit(solution)/shard_map/ppermute | solution.py:39
  47.9 3.2 %query.1 = (f32[128,256]{1,0:T(8,128)}, f32[96,256]{1,0:T(8,128)}, f32[96,256]{1,0:T(8,128)}, f32[96,256]{1,0:T(8,128)}, f32[96,256]{1,0:T(8,128)}, /*index=5*/f...) custom-call(f32[128,256]{1,0:T(8,128)} %queries.1, f32[128,256]{1,0:T(8,128)} %out_cot.1, ...), custom_call_target="tpu_custom_call" | custom-call | tf_op jit(solution)/shard_map/query/pallas_call | solution.py:236
  52.7 4.7 %forward.1 = (bf16[1024,256]{1,0:T(8,128)(2,1)}, bf16[1024,256]{1,0:T(8,128)(2,1)}, bf16[1024,256]{1,0:T(8,128)(2,1)}, bf16[1024,256]{1,0:T(8,128)(2,1)}, f32[5,...) custom-call(f32[3,32,256]{2,1,0:T(8,128)} %get-tuple-element.38.refs_0_.own.refs_1_, ...), custom_call_target="tpu_custom_call" | custom-call | tf_op jit(solution)/shard_map/forward/pallas_call | solution.py:236
  57.4 1.5 collective-permute-start.21
  58.9 2.8 %collective-permute-start.22 = (f32[8,256]{1,0:T(8,128)}, f32[8,256]{1,0:T(8,128)S(1)}, u32[]{:S(2)}, u32[]{:S(2)}) collective-permute-start(f32[8,256]{1,0:T(8,128)} %get-tuple-element.43), channel_id=1, source_target_pairs={{0,4},{1,5},{2,6},{3,7},{4,0},{5,1},{6,2},{7,3},{8,12},{9,13},{10,... | collective-permute-start | bytes 24584 | tf_op jit(solution)/shard_map/ppermute | solution.py:39
  62.6 3.4 %collective-permute-start.25 = (f32[2,32,256]{2,1,0:T(8,128)S(1)}, f32[2,32,256]{2,1,0:T(8,128)S(1)}, u32[]{:S(2)}, u32[]{:S(2)}) collective-permute-start(f32[2,32,256]{2,1,0:T(8,128)S(1)} %slice.12), channel_id=1, source_target_pairs={{0,8},{8,16},{16,24},{1,9},{9,17},{17,25},{2,10},{10,18},{18,26},{... | collective-permute-start | bytes 196616 | tf_op jit(solution)/shard_map/ppermute | solution.py:102
  67.0 1.7 %collective-permute-start.28 = (f32[96,256]{1,0:T(8,128)S(1)}, f32[96,256]{1,0:T(8,128)S(1)}, u32[]{:S(2)}, u32[]{:S(2)}) collective-permute-start(f32[96,256]{1,0:T(8,128)S(1)} %add.52), channel_id=1, source_target_pairs={{0,6},{1,7},{2,0},{3,1},{4,2},{5,3},{6,4},{7,5},{8,14},{9,15},{10,... | collective-permute-start | bytes 294920 | tf_op jit(solution)/shard_map/ppermute | solution.py:39
  68.7 1.9 %collective-permute-start.30 = (f32[96,256]{1,0:T(8,128)S(1)}, f32[96,256]{1,0:T(8,128)S(1)}, u32[]{:S(2)}, u32[]{:S(2)}) collective-permute-start(f32[96,256]{1,0:T(8,128)S(1)} %add.53), channel_id=1, source_target_pairs={{0,4},{1,5},{2,6},{3,7},{4,0},{5,1},{6,2},{7,3},{8,12},{9,13},{10,... | collective-permute-start | bytes 294920 | tf_op jit(solution)/shard_map/ppermute | solution.py:39
  72.5 7.5 %collective-permute-done.30.refs_14_.refs_17_.refs_20_.refs_23_ = f32[96,256]{1,0:T(8,128)S(1)} collective-permute-done((f32[96,256]{1,0:T(8,128)S(1)}, f32[96,256]{1,0:T(8,128)S(1)}, u32[]{:S(2)}, u32[]{:S(2)}) %collective-permute-start.30) | collective-permute-done | bytes 98336 | tf_op jit(solution)/shard_map/ppermute | solution.py:39
  80.7 2.6 %section.3 = (f32[104,256]{1,0:T(8,128)}, f32[8,256]{1,0:T(8,128)}) custom-call(s32[1]{0:T(128)} %bitcast.flag.refs_0_, f32[3,32,256]{2,1,0:T(8,128)} %get-tuple-element.38.refs_0_.own.refs_1_, f32[3,32,256]{2,1,0:T(8,128)} %get-tuple-element.42.refs_2_.refs_1_, f32[3,32,256]{2,1,0:T(8,128)} %get-tuple-element.40.last.refs_3_.refs_2_, f32[8,256]{1,0:T(8,128)} %copy-done.17, ...), custom_call_target="tpu_custom_call" | custom-call | tf_op jit(solution)/shard_map/section/pallas_call | solution.py:236
  87.9 2.7 %section.4 = (f32[104,256]{1,0:T(8,128)}, f32[8,256]{1,0:T(8,128)}) custom-call(s32[1]{0:T(128)} %bitcast.5.refs_0_, f32[3,32,256]{2,1,0:T(8,128)} %get-tuple-element.38.refs_0_.own.refs_1_, f32[3,32,256]{2,1,0:T(8,128)} %get-tuple-element.42.refs_2_.refs_1_, f32[3,32,256]{2,1,0:T(8,128)} %get-tuple-element.40.last.refs_3_.refs_2_, f32[8,256]{1,0:T(8,128)} %copy-done.17, ...), custom_call_target="tpu_custom_call" | custom-call | tf_op jit(solution)/shard_map/section/pallas_call | solution.py:236
  95.1 2.7 %section.5 = (f32[104,256]{1,0:T(8,128)}, f32[8,256]{1,0:T(8,128)}) custom-call(s32[1]{0:T(128)} %bitcast.6.refs_0_, f32[3,32,256]{2,1,0:T(8,128)} %get-tuple-element.38.refs_0_.own.refs_1_, f32[3,32,256]{2,1,0:T(8,128)} %get-tuple-element.42.refs_2_.refs_1_, f32[3,32,256]{2,1,0:T(8,128)} %get-tuple-element.40.last.refs_3_.refs_2_, f32[8,256]{1,0:T(8,128)} %copy-done.17, ...), custom_call_target="tpu_custom_call" | custom-call | tf_op jit(solution)/shard_map/section/pallas_call | solution.py:236
  103.1 20.9 %collective-permute-done.44 = f32[8,256]{1,0:T(8,128)S(1)} collective-permute-done((f32[8,256]{1,0:T(8,128)}, f32[8,256]{1,0:T(8,128)S(1)}, u32[]{:S(2)}, u32[]{:S(2)}) %collective-permute-start.44) | collective-permute-done | bytes 8224 | tf_op jit(solution)/shard_map/ppermute | solution.py:97
  127.6 4.9 %final.5 = (f32[256,128]{1,0:T(8,128)}, f32[32,256]{1,0:T(8,128)}) custom-call(s32[1]{0:T(128)} %constant.3.clone.1.refs_0_, f32[3,32,256]{2,1,0:T(8,128)} %get-tuple-element.38.refs_0_.own.refs_1_, f32[3,32,256]{2,1,0:T(8,128)} %get-tuple-element.42.refs_2_.refs_1_, f32[3,32,256]{2,1,0:T(8,128)} %get-tuple-element.40.last.refs_3_.refs_2_, ...), custom_call_target="tpu_custom_call" | custom-call | tf_op jit(solution)/shard_map/final/pallas_call | solution.py:236
  132.4 3.6 %all-to-all-start.1 = ((f32[8,32,128]{2,1,0:T(8,128)}), f32[8,32,128]{2,1,0:T(8,128)S(1)}, u32[]{:S(2)}, u32[]{:S(2)}) async-start(f32[8,32,128]{2,1,0:T(8,128)} %bitcast.15), calls=%async_computation.1 | async-start | bytes 262144 | tf_op jit(solution)/shard_map/all_to_all | solution.py:547
  136.1 2.0 %terms.1.refs_8_ = f32[3,32,256]{2,1,0:T(8,128)} custom-call(f32[3,32,256]{2,1,0:T(8,128)} %get-tuple-element.38.refs_0_.own.refs_1_, f32[3,32,256]{2,1,0:T(8,128)} %get-tuple-element.42.refs_2_.refs_1_, f32[3,32,256]{2,1,0:T(8,128)} %get-tuple-element.40.last.refs_3_.refs_2_, f32[8,256]{1,0:T(8,128)} %copy-done.17, f32[8,256]{1,0:T(8,128)} %copy-done.19, ...), custom_call_target="tpu_custom_call" | custom-call | tf_op jit(solution)/shard_map/terms/pallas_call | solution.py:236
  138.1 2.0 %collective-permute-start.48 = (f32[3,32,256]{2,1,0:T(8,128)}, f32[3,32,256]{2,1,0:T(8,128)S(1)}, u32[]{:S(2)}, u32[]{:S(2)}) collective-permute-start(f32[3,32,256]{2,1,0:T(8,128)} %terms.1.refs_8_), channel_id=1, source_target_pairs={{0,2},{1,3},{2,4},{3,5},{4,6},{5,7},{6,0},{7,1},{8,10},{9,11},{10,... | collective-permute-start | bytes 294920 | tf_op jit(solution)/shard_map/ppermute | solution.py:39
  140.1 2.4 %collective-permute-start.49 = (f32[3,32,256]{2,1,0:T(8,128)}, f32[3,32,256]{2,1,0:T(8,128)S(1)}, u32[]{:S(2)}, u32[]{:S(2)}) collective-permute-start(f32[3,32,256]{2,1,0:T(8,128)} %terms.1.refs_8_), channel_id=1, source_target_pairs={{0,4},{1,5},{2,6},{3,7},{4,0},{5,1},{6,2},{7,3},{8,12},{9,13},{10,... | collective-permute-start | bytes 294920 | tf_op jit(solution)/shard_map/ppermute | solution.py:39
  143.9 1.8 %collective-permute-done.48.refs_9_ = f32[3,32,256]{2,1,0:T(8,128)S(1)} collective-permute-done((f32[3,32,256]{2,1,0:T(8,128)}, f32[3,32,256]{2,1,0:T(8,128)S(1)}, u32[]{:S(2)}, u32[]{:S(2)}) %collective-permute-start.48) | collective-permute-done | bytes 98336 | tf_op jit(solution)/shard_map/ppermute | solution.py:39
  145.7 3.8 %collective-permute-done.49.refs_10_ = f32[3,32,256]{2,1,0:T(8,128)S(1)} collective-permute-done((f32[3,32,256]{2,1,0:T(8,128)}, f32[3,32,256]{2,1,0:T(8,128)S(1)}, u32[]{:S(2)}, u32[]{:S(2)}) %collective-permute-start.49) | collective-permute-done | bytes 98336 | tf_op jit(solution)/shard_map/ppermute | solution.py:39
  151.6 3.7 %token_.1 = (f32[128,256]{1,0:T(8,128)}, f32[128,256]{1,0:T(8,128)}, f32[1,128]{1,0:T(1,128)}, f32[3,32,256]{2,1,0:T(8,128)}) custom-call(f32[128,256]{1,0:T(8,128)} %keys.1, f32[128,256]{1,0:T(8,128)} %values.3, f32[1,128]{1,0:T(1,128)} %bitcast.18, f32[256,128]{1,0:T(8,128)} %bitcast.11, f32[32,256]{1,0:T(8,128)} %get-tuple-element.64.second, ...), custom_call_target="tpu_custom_call" | custom-call | tf_op jit(solution)/shard_map/token/pallas_call | solution.py:236
  (207 shorter events, 32.7 us)
Async XLA Ops:
  2.5 27.4 %all-to-all-start = ((f32[8,32,128]{2,1,0:T(8,128)}), f32[8,32,128]{2,1,0:T(8,128)S(1)}, u32[]{:S(2)}, u32[]{:S(2)}) async-start(f32[8,32,128]{2,1,0:T(8,128)} %bitcast.16), calls=%async_computation | async-start | bytes 262144 | tf_op jit(solution)/shard_map/all_to_all | solution.py:467
  9.0 10.5 %collective-permute-start.14 = (f32[128,256]{1,0:T(8,128)S(1)}, f32[128,256]{1,0:T(8,128)S(1)}, u32[]{:S(2)}, u32[]{:S(2)}) collective-permute-start(f32[128,256]{1,0:T(8,128)S(1)} %copy-done.22), channel_id=1, source_target_pairs={{0,2},{1,3},{2,4},{3,5},{4,6},{5,7},{6,0},{7,1},{8,10},{9,11},{10,... | collective-permute-start | bytes 393224 | tf_op jit(solution)/shard_map/ppermute | solution.py:39
  11.0 18.7 %collective-permute-start.15 = (f32[128,256]{1,0:T(8,128)S(1)}, f32[128,256]{1,0:T(8,128)S(1)}, u32[]{:S(2)}, u32[]{:S(2)}) collective-permute-start(f32[128,256]{1,0:T(8,128)S(1)} %copy-done.22), channel_id=1, source_target_pairs={{0,4},{1,5},{2,6},{3,7},{4,0},{5,1},{6,2},{7,3},{8,12},{9,13},{10,... | collective-permute-start | bytes 393224 | tf_op jit(solution)/shard_map/ppermute | solution.py:39
  13.4 16.4 %collective-permute-start.16 = (f32[128,256]{1,0:T(8,128)S(1)}, f32[128,256]{1,0:T(8,128)S(1)}, u32[]{:S(2)}, u32[]{:S(2)}) collective-permute-start(f32[128,256]{1,0:T(8,128)S(1)} %copy-done.22), channel_id=1, source_target_pairs={{0,6},{1,7},{2,0},{3,1},{4,2},{5,3},{6,4},{7,5},{8,14},{9,15},{10,... | collective-permute-start | bytes 393224 | tf_op jit(solution)/shard_map/ppermute | solution.py:39
  14.8 17.5 %collective-permute-start.17 = (f32[128,256]{1,0:T(8,128)S(1)}, f32[128,256]{1,0:T(8,128)S(1)}, u32[]{:S(2)}, u32[]{:S(2)}) collective-permute-start(f32[128,256]{1,0:T(8,128)S(1)} %copy-done.22), channel_id=1, source_target_pairs={{0,1},{1,0},{2,3},{3,2},{4,5},{5,4},{6,7},{7,6},{8,9},{9,8},{10,11... | collective-permute-start | bytes 393224 | tf_op jit(solution)/shard_map/ppermute | solution.py:44
  14.8 21.3 %collective-permute-start.7 = (f32[128,256]{1,0:T(8,128)S(1)}, f32[128,256]{1,0:T(8,128)S(1)}, u32[]{:S(2)}, u32[]{:S(2)}) collective-permute-start(f32[128,256]{1,0:T(8,128)S(1)} %copy-done.6), channel_id=1, source_target_pairs={{0,2},{1,3},{2,4},{3,5},{4,6},{5,7},{6,0},{7,1},{8,10},{9,11},{10,... | collective-permute-start | bytes 393224 | tf_op jit(solution)/shard_map/ppermute | solution.py:39
  19.5 16.9 %collective-permute-start.8 = (f32[128,256]{1,0:T(8,128)S(1)}, f32[128,256]{1,0:T(8,128)S(1)}, u32[]{:S(2)}, u32[]{:S(2)}) collective-permute-start(f32[128,256]{1,0:T(8,128)S(1)} %copy-done.6), channel_id=1, source_target_pairs={{0,4},{1,5},{2,6},{3,7},{4,0},{5,1},{6,2},{7,3},{8,12},{9,13},{10,... | collective-permute-start | bytes 393224 | tf_op jit(solution)/shard_map/ppermute | solution.py:39
  29.8 7.2 %collective-permute-start.9 = (f32[128,256]{1,0:T(8,128)S(1)}, f32[128,256]{1,0:T(8,128)S(1)}, u32[]{:S(2)}, u32[]{:S(2)}) collective-permute-start(f32[128,256]{1,0:T(8,128)S(1)} %copy-done.6), channel_id=1, source_target_pairs={{0,6},{1,7},{2,0},{3,1},{4,2},{5,3},{6,4},{7,5},{8,14},{9,15},{10,... | collective-permute-start | bytes 393224 | tf_op jit(solution)/shard_map/ppermute | solution.py:39
  29.8 10.0 %collective-permute-start.10 = (f32[128,256]{1,0:T(8,128)S(1)}, f32[128,256]{1,0:T(8,128)S(1)}, u32[]{:S(2)}, u32[]{:S(2)}) collective-permute-start(f32[128,256]{1,0:T(8,128)S(1)} %copy-done.6), channel_id=1, source_target_pairs={{0,1},{1,0},{2,3},{3,2},{4,5},{5,4},{6,7},{7,6},{8,9},{9,8},{10,11... | collective-permute-start | bytes 393224 | tf_op jit(solution)/shard_map/ppermute | solution.py:44
  32.3 7.5 %collective-permute-start = (f32[3,32,256]{2,1,0:T(8,128)}, f32[3,32,256]{2,1,0:T(8,128)S(1)}, u32[]{:S(2)}, u32[]{:S(2)}) collective-permute-start(f32[3,32,256]{2,1,0:T(8,128)} %get-tuple-element.38.refs_0_.own.refs_1_), channel_id=1, source_target_pairs={{0,2},{1,3},{2,4},{3,5},{4,6},{5,7},{6,0},{7,1},{8,10},{9,11},{10,... | collective-permute-start | bytes 294920 | tf_op jit(solution)/shard_map/ppermute | solution.py:39
  36.1 9.8 %collective-permute-start.18 = (f32[128,256]{1,0:T(8,128)S(1)}, f32[128,256]{1,0:T(8,128)S(1)}, u32[]{:S(2)}, u32[]{:S(2)}) collective-permute-start(f32[128,256]{1,0:T(8,128)S(1)} %collective-permute-done.14.refs_9_), channel_id=1, source_target_pairs={{0,1},{1,0},{2,3},{3,2},{4,5},{5,4},{6,7},{7,6},{8,9},{9,8},{10,11... | collective-permute-start | bytes 393224 | tf_op jit(solution)/shard_map/ppermute | solution.py:44
  36.3 8.6 %collective-permute-start.1 = (f32[3,32,256]{2,1,0:T(8,128)}, f32[3,32,256]{2,1,0:T(8,128)S(1)}, u32[]{:S(2)}, u32[]{:S(2)}) collective-permute-start(f32[3,32,256]{2,1,0:T(8,128)} %get-tuple-element.38.refs_0_.own.refs_1_), channel_id=1, source_target_pairs={{0,4},{1,5},{2,6},{3,7},{4,0},{5,1},{6,2},{7,3},{8,12},{9,13},{10,... | collective-permute-start | bytes 294920 | tf_op jit(solution)/shard_map/ppermute | solution.py:39
  37.0 9.0 %collective-permute-start.2 = (f32[3,32,256]{2,1,0:T(8,128)}, f32[3,32,256]{2,1,0:T(8,128)S(1)}, u32[]{:S(2)}, u32[]{:S(2)}) collective-permute-start(f32[3,32,256]{2,1,0:T(8,128)} %get-tuple-element.38.refs_0_.own.refs_1_), channel_id=1, source_target_pairs={{0,6},{1,7},{2,0},{3,1},{4,2},{5,3},{6,4},{7,5},{8,14},{9,15},{10,... | collective-permute-start | bytes 294920 | tf_op jit(solution)/shard_map/ppermute | solution.py:39
  39.8 6.6 %collective-permute-start.3 = (f32[3,32,256]{2,1,0:T(8,128)}, f32[3,32,256]{2,1,0:T(8,128)S(1)}, u32[]{:S(2)}, u32[]{:S(2)}) collective-permute-start(f32[3,32,256]{2,1,0:T(8,128)} %get-tuple-element.38.refs_0_.own.refs_1_), channel_id=1, source_target_pairs={{0,1},{1,0},{2,3},{3,2},{4,5},{5,4},{6,7},{7,6},{8,9},{9,8},{10,11... | collective-permute-start | bytes 294920 | tf_op jit(solution)/shard_map/ppermute | solution.py:44
  39.9 6.7 %collective-permute-start.4 = (f32[3,32,256]{2,1,0:T(8,128)S(1)}, f32[3,32,256]{2,1,0:T(8,128)S(1)}, u32[]{:S(2)}, u32[]{:S(2)}) collective-permute-start(f32[3,32,256]{2,1,0:T(8,128)S(1)} %collective-permute-done.refs_1_), channel_id=1, source_target_pairs={{0,1},{1,0},{2,3},{3,2},{4,5},{5,4},{6,7},{7,6},{8,9},{9,8},{10,11... | collective-permute-start | bytes 294920 | tf_op jit(solution)/shard_map/ppermute | solution.py:44
  51.2 10.5 %collective-permute-start.27 = (f32[96,256]{1,0:T(8,128)}, f32[96,256]{1,0:T(8,128)S(1)}, u32[]{:S(2)}, u32[]{:S(2)}) collective-permute-start(f32[96,256]{1,0:T(8,128)} %get-tuple-element.52), channel_id=1, source_target_pairs={{0,1},{1,0},{2,3},{3,2},{4,5},{5,4},{6,7},{7,6},{8,9},{9,8},{10,11... | collective-permute-start | bytes 294920 | tf_op jit(solution)/shard_map/ppermute | solution.py:44
  51.5 11.1 %collective-permute-start.29 = (f32[96,256]{1,0:T(8,128)}, f32[96,256]{1,0:T(8,128)S(1)}, u32[]{:S(2)}, u32[]{:S(2)}) collective-permute-start(f32[96,256]{1,0:T(8,128)} %get-tuple-element.54), channel_id=1, source_target_pairs={{0,1},{1,0},{2,3},{3,2},{4,5},{5,4},{6,7},{7,6},{8,9},{9,8},{10,11... | collective-permute-start | bytes 294920 | tf_op jit(solution)/shard_map/ppermute | solution.py:44
  51.8 14.3 %collective-permute-start.31 = (f32[96,256]{1,0:T(8,128)}, f32[96,256]{1,0:T(8,128)S(1)}, u32[]{:S(2)}, u32[]{:S(2)}) collective-permute-start(f32[96,256]{1,0:T(8,128)} %get-tuple-element.56), channel_id=1, source_target_pairs={{0,1},{1,0},{2,3},{3,2},{4,5},{5,4},{6,7},{7,6},{8,9},{9,8},{10,11... | collective-permute-start | bytes 294920 | tf_op jit(solution)/shard_map/ppermute | solution.py:44
  57.4 9.6 %collective-permute-start.21 = (f32[8,256]{1,0:T(8,128)}, f32[8,256]{1,0:T(8,128)S(1)}, u32[]{:S(2)}, u32[]{:S(2)}) collective-permute-start(f32[8,256]{1,0:T(8,128)} %get-tuple-element.43), channel_id=1, source_target_pairs={{0,2},{1,3},{2,4},{3,5},{4,6},{5,7},{6,0},{7,1},{8,10},{9,11},{10,... | collective-permute-start | bytes 24584 | tf_op jit(solution)/shard_map/ppermute | solution.py:39
  58.9 9.7 %collective-permute-start.22 = (f32[8,256]{1,0:T(8,128)}, f32[8,256]{1,0:T(8,128)S(1)}, u32[]{:S(2)}, u32[]{:S(2)}) collective-permute-start(f32[8,256]{1,0:T(8,128)} %get-tuple-element.43), channel_id=1, source_target_pairs={{0,4},{1,5},{2,6},{3,7},{4,0},{5,1},{6,2},{7,3},{8,12},{9,13},{10,... | collective-permute-start | bytes 24584 | tf_op jit(solution)/shard_map/ppermute | solution.py:39
  61.7 8.8 %collective-permute-start.23 = (f32[8,256]{1,0:T(8,128)}, f32[8,256]{1,0:T(8,128)S(1)}, u32[]{:S(2)}, u32[]{:S(2)}) collective-permute-start(f32[8,256]{1,0:T(8,128)} %get-tuple-element.43), channel_id=1, source_target_pairs={{0,6},{1,7},{2,0},{3,1},{4,2},{5,3},{6,4},{7,5},{8,14},{9,15},{10,... | collective-permute-start | bytes 24584 | tf_op jit(solution)/shard_map/ppermute | solution.py:39
  62.6 9.3 %collective-permute-start.25 = (f32[2,32,256]{2,1,0:T(8,128)S(1)}, f32[2,32,256]{2,1,0:T(8,128)S(1)}, u32[]{:S(2)}, u32[]{:S(2)}) collective-permute-start(f32[2,32,256]{2,1,0:T(8,128)S(1)} %slice.12), channel_id=1, source_target_pairs={{0,8},{8,16},{16,24},{1,9},{9,17},{17,25},{2,10},{10,18},{18,26},{... | collective-permute-start | bytes 196616 | tf_op jit(solution)/shard_map/ppermute | solution.py:102
  68.7 11.3 %collective-permute-start.30 = (f32[96,256]{1,0:T(8,128)S(1)}, f32[96,256]{1,0:T(8,128)S(1)}, u32[]{:S(2)}, u32[]{:S(2)}) collective-permute-start(f32[96,256]{1,0:T(8,128)S(1)} %add.53), channel_id=1, source_target_pairs={{0,4},{1,5},{2,6},{3,7},{4,0},{5,1},{6,2},{7,3},{8,12},{9,13},{10,... | collective-permute-start | bytes 294920 | tf_op jit(solution)/shard_map/ppermute | solution.py:39
  70.5 9.5 %collective-permute-start.32 = (f32[96,256]{1,0:T(8,128)S(1)}, f32[96,256]{1,0:T(8,128)S(1)}, u32[]{:S(2)}, u32[]{:S(2)}) collective-permute-start(f32[96,256]{1,0:T(8,128)S(1)} %add.54), channel_id=1, source_target_pairs={{0,2},{1,3},{2,4},{3,5},{4,6},{5,7},{6,0},{7,1},{8,10},{9,11},{10,... | collective-permute-start | bytes 294920 | tf_op jit(solution)/shard_map/ppermute | solution.py:39
  97.9 27.8 %collective-permute-start.43 = (f32[104,256]{1,0:T(8,128)}, f32[104,256]{1,0:T(8,128)S(1)}, u32[]{:S(2)}, u32[]{:S(2)}) collective-permute-start(f32[104,256]{1,0:T(8,128)} %get-tuple-element.61), channel_id=1, source_target_pairs={{8,0},{9,1},{10,2},{11,3},{12,4},{13,5},{14,6},{15,7}} | collective-permute-start | bytes 319496 | tf_op jit(solution)/shard_map/ppermute | solution.py:97
  99.2 24.8 %collective-permute-start.44 = (f32[8,256]{1,0:T(8,128)}, f32[8,256]{1,0:T(8,128)S(1)}, u32[]{:S(2)}, u32[]{:S(2)}) collective-permute-start(f32[8,256]{1,0:T(8,128)} %get-tuple-element.62), channel_id=1, source_target_pairs={{8,2},{9,3},{10,4},{11,5},{12,6},{13,7},{14,0},{15,1}} | collective-permute-start | bytes 24584 | tf_op jit(solution)/shard_map/ppermute | solution.py:97
  100.5 24.4 %collective-permute-start.45 = (f32[8,256]{1,0:T(8,128)}, f32[8,256]{1,0:T(8,128)S(1)}, u32[]{:S(2)}, u32[]{:S(2)}) collective-permute-start(f32[8,256]{1,0:T(8,128)} %get-tuple-element.62), channel_id=1, source_target_pairs={{8,4},{9,5},{10,6},{11,7},{12,0},{13,1},{14,2},{15,3}} | collective-permute-start | bytes 24584 | tf_op jit(solution)/shard_map/ppermute | solution.py:97
  101.8 23.9 %collective-permute-start.46 = (f32[8,256]{1,0:T(8,128)}, f32[8,256]{1,0:T(8,128)S(1)}, u32[]{:S(2)}, u32[]{:S(2)}) collective-permute-start(f32[8,256]{1,0:T(8,128)} %get-tuple-element.62), channel_id=1, source_target_pairs={{8,6},{9,7},{10,0},{11,1},{12,2},{13,3},{14,4},{15,5}} | collective-permute-start | bytes 24584 | tf_op jit(solution)/shard_map/ppermute | solution.py:97
  132.4 18.5 %all-to-all-start.1 = ((f32[8,32,128]{2,1,0:T(8,128)}), f32[8,32,128]{2,1,0:T(8,128)S(1)}, u32[]{:S(2)}, u32[]{:S(2)}) async-start(f32[8,32,128]{2,1,0:T(8,128)} %bitcast.15), calls=%async_computation.1 | async-start | bytes 262144 | tf_op jit(solution)/shard_map/all_to_all | solution.py:547
  138.1 7.7 %collective-permute-start.48 = (f32[3,32,256]{2,1,0:T(8,128)}, f32[3,32,256]{2,1,0:T(8,128)S(1)}, u32[]{:S(2)}, u32[]{:S(2)}) collective-permute-start(f32[3,32,256]{2,1,0:T(8,128)} %terms.1.refs_8_), channel_id=1, source_target_pairs={{0,2},{1,3},{2,4},{3,5},{4,6},{5,7},{6,0},{7,1},{8,10},{9,11},{10,... | collective-permute-start | bytes 294920 | tf_op jit(solution)/shard_map/ppermute | solution.py:39
  140.1 9.4 %collective-permute-start.49 = (f32[3,32,256]{2,1,0:T(8,128)}, f32[3,32,256]{2,1,0:T(8,128)S(1)}, u32[]{:S(2)}, u32[]{:S(2)}) collective-permute-start(f32[3,32,256]{2,1,0:T(8,128)} %terms.1.refs_8_), channel_id=1, source_target_pairs={{0,4},{1,5},{2,6},{3,7},{4,0},{5,1},{6,2},{7,3},{8,12},{9,13},{10,... | collective-permute-start | bytes 294920 | tf_op jit(solution)/shard_map/ppermute | solution.py:39
  142.4 7.2 %collective-permute-start.50 = (f32[3,32,256]{2,1,0:T(8,128)}, f32[3,32,256]{2,1,0:T(8,128)S(1)}, u32[]{:S(2)}, u32[]{:S(2)}) collective-permute-start(f32[3,32,256]{2,1,0:T(8,128)} %terms.1.refs_8_), channel_id=1, source_target_pairs={{0,6},{1,7},{2,0},{3,1},{4,2},{5,3},{6,4},{7,5},{8,14},{9,15},{10,... | collective-permute-start | bytes 294920 | tf_op jit(solution)/shard_map/ppermute | solution.py:39
  (78 other events, 326.0 us)
